TPU v7x, 128 devices: a whole 4x4x4 slice. The times are simulated.
128 devices in a mesh: inlet: 4 (over y), row: 32 (over z, x, core).
Axes of the slice: x: 4, y: 4, z: 4, core: 2. Of those that a mesh axis runs over, the one named last changes fastest.
Arguments:
- coeffs: float32 [4, 1024, 1024], P('inlet', 'row'), may hold values from -6 to 6
- basis: float32 [4, 8192, 3, 1024], P('inlet', 'row'), may hold values from -0.1875 to 0.1875
- route: int32 [32768, 1], P(('inlet', 'row')), may hold values from 0 to 127; in each aligned block of 256 rows (0 to 255, 256 to 511, ...) at most 3 rows name the same one
Outputs:
- inflow: bfloat16 [49152, 3, 1024], P(('inlet', 'row'))
Inputs may be any that keep to these rules, and one draw needn't show every extreme that they name: `route`: among the rows of one device, no owner is named more than 3 times, a bound that some block reaches.
All inputs are finite; a program needn't handle non-finite values.
Results may differ from a plain program's by a relative error of at most 0.001.
Values may be sent and summed in bfloat16 or wider, within the bound.
No kernel may reach another device: no remote copies, remote signals or barrier semaphores. Data moves between devices by JAX's collectives and lax.ppermute only.
A program may use at most 64 MiB of HBM per device.

v0:
```python
import functools

import jax
import jax.numpy as jnp
from jax import lax
from jax.experimental import pallas as pl
from jax.experimental.pallas import tpu as pltpu
from jax.sharding import PartitionSpec as P


SIDE = 4
HOPS = (0, 1, 3, 2)
DEVICES = 128
CAP = 3
COMPS = 3
LANES = 128


def place(z, x, c):
    return (z * SIDE + x) * 2 + c


def turn(array, first, second, k):
    pairs = []
    for z in range(SIDE):
        for x in range(SIDE):
            for c in range(2):
                axis = (first, second)[c]
                tz = (z + k) % SIDE if axis == "z" else z
                tx = (x + k) % SIDE if axis == "x" else x
                pairs.append((place(z, x, c), place(tz, tx, c)))
    return lax.ppermute(array, "row", pairs)


def partner(array):
    return lax.ppermute(array, "row", [(i, i ^ 1) for i in range(2 * SIDE * SIDE)])


def split(value):
    high = value.astype(jnp.bfloat16)
    return high, (value - high.astype(jnp.float32)).astype(jnp.bfloat16)


def prepare_kernel(points, route, basis, high, low, picks, base, sems):
    copies = [
        pltpu.make_async_copy(basis.at[comp], base.at[comp], sems.at[comp]) for comp in range(COMPS)
    ]
    for copy in copies:
        copy.start()
    mine = lax.broadcasted_iota(jnp.int32, (DEVICES, points), 0) == route[...]
    before = lax.broadcasted_iota(jnp.int32, (points, points), 0) < lax.broadcasted_iota(
        jnp.int32, (points, points), 1
    )
    count = jnp.dot(
        jnp.where(mine, 1.0, 0.0).astype(jnp.bfloat16),
        jnp.where(before, 1.0, 0.0).astype(jnp.bfloat16),
        preferred_element_type=jnp.float32,
    )
    for r in range(CAP):
        picks[pl.ds(r * DEVICES, DEVICES), :] = jnp.where(
            mine & (count == float(r)), 1.0, 0.0
        ).astype(jnp.bfloat16)
    for comp in range(COMPS):
        copies[comp].wait()
        high[pl.ds(comp * points, points), :], low[pl.ds(comp * points, points), :] = split(
            base[comp]
        )


def prepare(route, basis):
    comps, points, modes = basis.shape
    whole = pl.BlockSpec(memory_space=pltpu.VMEM)
    half = jax.ShapeDtypeStruct((comps * points, modes), jnp.bfloat16)
    return pl.pallas_call(
        functools.partial(prepare_kernel, points),
        out_shape=(half, half, jax.ShapeDtypeStruct((CAP * DEVICES, points), jnp.bfloat16)),
        in_specs=[whole, pl.BlockSpec(memory_space=pl.ANY)],
        out_specs=(whole, whole, whole),
        scratch_shapes=[
            pltpu.VMEM((comps, points, modes), jnp.float32),
            pltpu.SemaphoreType.DMA((comps,)),
        ],
        compiler_params=pltpu.CompilerParams(vmem_limit_bytes=12 << 20),
        cost_estimate=pl.CostEstimate(flops=20_000_000, bytes_accessed=8 << 20, transcendentals=0),
        name="prepare",
    )(route, basis)


def build_kernel(layout, rows, coord, *refs):
    pieces = refs[: len(layout)]
    high_in, low_in, picks_in, message = refs[len(layout) : len(layout) + 4]
    coef, high, low, picks, spread, packed, base_sems, sems, out_sems = refs[len(layout) + 4 :]
    z, x, c = coord[0], coord[1], coord[2]
    fixed = [
        pltpu.make_async_copy(source, target, base_sems.at[i])
        for i, (source, target) in enumerate(((high_in, high), (low_in, low), (picks_in, picks)))
    ]
    fixed[0].start()
    for piece, (side, outer, inners) in zip(pieces, layout):
        core = c if side == 0 else 1 - c
        for i, inner in enumerate(inners):
            dz = jnp.where(core == 0, inner, outer)
            dx = jnp.where(core == 0, outer, inner)
            sz = lax.rem(z - dz + SIDE, SIDE)
            sx = lax.rem(x - dx + SIDE, SIDE)
            start = pl.multiple_of(((sz * SIDE + sx) * 2 + core) * rows, rows)
            pltpu.make_async_copy(
                piece.at[i], coef.at[pl.ds(start, rows)], sems.at[sz]
            ).start()
    fixed[1].start()
    fixed[2].start()

    points = picks.shape[1]
    width = 8 * rows
    blocks = width // LANES
    contract = functools.partial(
        lax.dot_general,
        dimension_numbers=(((1,), (1,)), ((), ())),
        preferred_element_type=jnp.float32,
    )
    for copy in fixed:
        copy.wait()

    def step(i, _):
        here = coef.at[pl.ds(pl.multiple_of(i * width, width), width)]
        pltpu.make_async_copy(here, here, sems.at[i]).wait()
        top, rest = split(here[...])
        value = contract(high[...], rest)
        value = value + contract(low[...], top)
        value = value + contract(high[...], top)
        value = value.astype(jnp.bfloat16)
        for comp in range(COMPS):
            moved = jnp.dot(
                picks[...],
                value[comp * points : (comp + 1) * points, :],
                preferred_element_type=jnp.float32,
            )
            for r in range(CAP):
                for half in range(blocks):
                    spread[r * COMPS + comp, pl.ds(i * blocks + half, DEVICES, stride=8), :] = (
                        moved[
                            r * DEVICES : (r + 1) * DEVICES, half * LANES : (half + 1) * LANES
                        ]
                    )
        return 0

    lax.fori_loop(0, SIDE, step, 0)
    part = DEVICES // 8

    def leave(i):
        some = pl.ds(i * part, part)
        return pltpu.make_async_copy(packed.at[some], message.at[some], out_sems.at[i])

    def pack(i, _):
        for row in range(CAP * COMPS):
            packed[pl.ds(i * part, part), pl.ds(row * 8, 8), :] = (
                spread[row, pl.ds(pl.multiple_of(i * part * 8, part * 8), part * 8), :]
                .reshape(part, 8, LANES)
                .astype(jnp.bfloat16)
            )
        leave(i).start()
        return 0

    lax.fori_loop(0, 8, pack, 0)
    for i in range(8):
        leave(i).wait()


def build(coord, pieces, layout, high, low, picks):
    rows, modes = pieces[0].shape[1:]
    anywhere = pl.BlockSpec(memory_space=pl.ANY)
    sent = (DEVICES, CAP * COMPS * 8, LANES)
    return pl.pallas_call(
        functools.partial(build_kernel, layout, rows),
        out_shape=jax.ShapeDtypeStruct(sent, jnp.bfloat16),
        in_specs=[pl.BlockSpec(memory_space=pltpu.SMEM)] + [anywhere] * (len(pieces) + 3),
        out_specs=anywhere,
        scratch_shapes=[
            pltpu.VMEM((32 * rows, modes), jnp.float32),
            pltpu.VMEM(high.shape, jnp.bfloat16),
            pltpu.VMEM(low.shape, jnp.bfloat16),
            pltpu.VMEM(picks.shape, jnp.bfloat16),
            pltpu.VMEM((CAP * COMPS, DEVICES * 8, LANES), jnp.float32),
            pltpu.VMEM(sent, jnp.bfloat16),
            pltpu.SemaphoreType.DMA((3,)),
            pltpu.SemaphoreType.DMA((SIDE,)),
            pltpu.SemaphoreType.DMA((8,)),
        ],
        compiler_params=pltpu.CompilerParams(vmem_limit_bytes=32 << 20),
        name="build",
    )(coord, *pieces, high, low, picks)


def settle_kernel(count, received, out, arrived, wide, narrow, ready, in_sems, out_sems):
    parts = DEVICES // count

    def enter(i):
        some = pl.ds(i * count, count)
        return pltpu.make_async_copy(received.at[some], arrived.at[some], in_sems.at[i])

    def lines(i):
        return pl.ds(pl.multiple_of(i * count * CAP, count * CAP), count * CAP)

    def leave(i):
        return pltpu.make_async_copy(ready.at[:, lines(i)], out.at[:, lines(i)], out_sems.at[i])

    for i in range(parts):
        enter(i).start()

    def step(i, _):
        enter(i).wait()
        wide[...] = (
            arrived[pl.ds(i * count, count)].reshape(count * 72, LANES).astype(jnp.float32)
        )
        for comp in range(COMPS):
            for j in range(8):
                for r in range(CAP):
                    narrow[comp * 8 + j, pl.ds(r, count, stride=CAP), :] = wide[
                        pl.ds((r * COMPS + comp) * 8 + j, count, stride=72), :
                    ]
        for comp in range(COMPS):
            for j in range(8):
                ready[comp, lines(i), j * LANES : (j + 1) * LANES] = narrow[comp * 8 + j].astype(
                    jnp.bfloat16
                )
        leave(i).start()
        return 0

    lax.fori_loop(0, parts, step, 0)
    for i in range(parts):
        leave(i).wait()


def settle(received):
    count = 16
    anywhere = pl.BlockSpec(memory_space=pl.ANY)
    shape = (COMPS, DEVICES * CAP, 8 * LANES)
    return pl.pallas_call(
        functools.partial(settle_kernel, count),
        out_shape=jax.ShapeDtypeStruct(shape, jnp.bfloat16),
        in_specs=[anywhere],
        out_specs=anywhere,
        scratch_shapes=[
            pltpu.VMEM(received.shape, jnp.bfloat16),
            pltpu.VMEM((count * 72, LANES), jnp.float32),
            pltpu.VMEM((COMPS * 8, count * CAP, LANES), jnp.float32),
            pltpu.VMEM(shape, jnp.bfloat16),
            pltpu.SemaphoreType.DMA((DEVICES // count,)),
            pltpu.SemaphoreType.DMA((DEVICES // count,)),
        ],
        compiler_params=pltpu.CompilerParams(vmem_limit_bytes=24 << 20),
        name="settle",
    )(received)


def steps(coeffs, basis, route):
    high, low, picks = prepare(route.reshape(1, -1), jnp.transpose(basis[0], (1, 0, 2)))
    own = coeffs[0]
    near = [own]
    for k in HOPS[1:]:
        near.append(turn(own, "z", "x", k))
    line = jnp.stack(near)
    mate = partner(line)
    pieces, layout = [line, mate], [(0, 0, HOPS), (1, 0, HOPS)]

    def far(array, first, second, k, side, inners):
        moved = turn(array, first, second, k)
        pieces.extend([moved, partner(moved)])
        layout.extend([(side, k, inners), (1 - side, k, inners)])

    far(line, "x", "z", 1, 0, HOPS)
    far(line, "x", "z", 3, 0, HOPS)
    far(line[:2], "x", "z", 2, 0, HOPS[:2])
    far(mate[2:], "z", "x", 2, 1, HOPS[2:])
    row = lax.axis_index("row")
    coord = jnp.stack([row // 8, row // 2 % 4, row % 2]).astype(jnp.int32)
    message = build(coord, pieces, tuple(layout), high, low, picks)
    received = lax.all_to_all(message, ("inlet", "row"), split_axis=0, concat_axis=0, tiled=True)
    return jnp.transpose(settle(received), (1, 0, 2))


def solution(mesh):
    in_specs = (P("inlet", "row", None), P("inlet", "row", None, None), P(("inlet", "row"), None))
    out_specs = P(("inlet", "row"), None, None)
    return jax.shard_map(steps, mesh=mesh, in_specs=in_specs, out_specs=out_specs, check_vma=False)
```

profile of v0, /device:TPU:1, one launch (start us, length us, event | category | flops | bytes accessed | tf_op | source)
XLA Modules:
  0.0 97.1 jit_solution(10157369741202369555)
XLA Ops:
  0.0 3.6 %collective-permute-start.2 = (f32[32,1024]{1,0:T(8,128)}, f32[32,1024]{1,0:T(8,128)S(1)}, u32[]{:S(2)}, u32[]{:S(2)}) collective-permute-start(f32[32,1024]{1,0:T(8,128)} %bitcast.14), channel_id=1, source_target_pairs={{0,16},{1,5},{2,18},{3,7},{4,20},{5,1},{6,22},{7,3},{8,24},{9,13},... | collective-permute-start | bytes 393224 | tf_op jit(solution)/shard_map/ppermute | solution.py:32
  3.6 0.9 collective-permute-start.1
  4.4 0.6 collective-permute-start
  5.0 1.1 %collective-permute-done.2 = f32[32,1024]{1,0:T(8,128)S(1)} collective-permute-done((f32[32,1024]{1,0:T(8,128)}, f32[32,1024]{1,0:T(8,128)S(1)}, u32[]{:S(2)}, u32[]{:S(2)}) %collective-permute-start.2) | collective-permute-done | bytes 131104 | tf_op jit(solution)/shard_map/ppermute | solution.py:32
  6.1 2.0 %collective-permute-done.1 = f32[32,1024]{1,0:T(8,128)S(1)} collective-permute-done((f32[32,1024]{1,0:T(8,128)}, f32[32,1024]{1,0:T(8,128)S(1)}, u32[]{:S(2)}, u32[]{:S(2)}) %collective-permute-start.1) | collective-permute-done | bytes 131104 | tf_op jit(solution)/shard_map/ppermute | solution.py:32
  8.1 1.5 %collective-permute-done = f32[32,1024]{1,0:T(8,128)S(1)} collective-permute-done((f32[32,1024]{1,0:T(8,128)}, f32[32,1024]{1,0:T(8,128)S(1)}, u32[]{:S(2)}, u32[]{:S(2)}) %collective-permute-start) | collective-permute-done | bytes 131104 | tf_op jit(solution)/shard_map/ppermute | solution.py:32
  9.7 0.9 pad_maximum_fusion.refs_0_
  10.6 3.8 %collective-permute-start.6 = (f32[4,32,1024]{2,1,0:T(8,128)S(1)}, f32[4,32,1024]{2,1,0:T(8,128)S(1)}, u32[]{:S(2)}, u32[]{:S(2)}) collective-permute-start(f32[4,32,1024]{2,1,0:T(8,128)S(1)} %pad_maximum_fusion.refs_0_), channel_id=1, source_target_pairs={{0,6},{1,25},{2,0},{3,27},{4,2},{5,29},{6,4},{7,31},{8,14},{9,1},{... | collective-permute-start | bytes 1572872 | tf_op jit(solution)/shard_map/ppermute | solution.py:32
  14.4 0.0 collective-permute-start.4
  14.4 1.8 %collective-permute-start.3 = (f32[4,32,1024]{2,1,0:T(8,128)S(1)}, f32[4,32,1024]{2,1,0:T(8,128)S(1)}, u32[]{:S(2)}, u32[]{:S(2)}) collective-permute-start(f32[4,32,1024]{2,1,0:T(8,128)S(1)} %pad_maximum_fusion.refs_0_), channel_id=1, source_target_pairs={{0,1},{1,0},{2,3},{3,2},{4,5},{5,4},{6,7},{7,6},{8,9},{9,8},{10,11... | collective-permute-start | bytes 1572872 | tf_op jit(solution)/shard_map/ppermute | solution.py:36
  16.3 0.9 pad_maximum_fusion.1
  17.2 1.0 collective-permute-start.8
  18.1 5.2 %collective-permute-done.6.refs_4_ = f32[4,32,1024]{2,1,0:T(8,128)S(1)} collective-permute-done((f32[4,32,1024]{2,1,0:T(8,128)S(1)}, f32[4,32,1024]{2,1,0:T(8,128)S(1)}, u32[]{:S(2)}, u32[]{:S(2)}) %collective-permute-start.6) | collective-permute-done | bytes 524320 | tf_op jit(solution)/shard_map/ppermute | solution.py:32
  23.4 2.4 %collective-permute-start.7 = (f32[4,32,1024]{2,1,0:T(8,128)S(1)}, f32[4,32,1024]{2,1,0:T(8,128)S(1)}, u32[]{:S(2)}, u32[]{:S(2)}) collective-permute-start(f32[4,32,1024]{2,1,0:T(8,128)S(1)} %collective-permute-done.6.refs_4_), channel_id=1, source_target_pairs={{0,1},{1,0},{2,3},{3,2},{4,5},{5,4},{6,7},{7,6},{8,9},{9,8},{10,11... | collective-permute-start | bytes 1572872 | tf_op jit(solution)/shard_map/ppermute | solution.py:36
  25.8 1.0 %collective-permute-done.4.refs_2_ = f32[4,32,1024]{2,1,0:T(8,128)S(1)} collective-permute-done((f32[4,32,1024]{2,1,0:T(8,128)S(1)}, f32[4,32,1024]{2,1,0:T(8,128)S(1)}, u32[]{:S(2)}, u32[]{:S(2)}) %collective-permute-start.4) | collective-permute-done | bytes 524320 | tf_op jit(solution)/shard_map/ppermute | solution.py:32
  26.8 2.7 %collective-permute-start.5 = (f32[4,32,1024]{2,1,0:T(8,128)S(1)}, f32[4,32,1024]{2,1,0:T(8,128)S(1)}, u32[]{:S(2)}, u32[]{:S(2)}) collective-permute-start(f32[4,32,1024]{2,1,0:T(8,128)S(1)} %collective-permute-done.4.refs_2_), channel_id=1, source_target_pairs={{0,1},{1,0},{2,3},{3,2},{4,5},{5,4},{6,7},{7,6},{8,9},{9,8},{10,11... | collective-permute-start | bytes 1572872 | tf_op jit(solution)/shard_map/ppermute | solution.py:36
  29.5 0.0 collective-permute-done.3.refs_1_
  29.5 0.1 collective-permute-start.10
  29.6 0.0 collective-permute-done.8.refs_6_
  29.6 1.1 %collective-permute-start.9 = (f32[2,32,1024]{2,1,0:T(8,128)S(1)}, f32[2,32,1024]{2,1,0:T(8,128)}, u32[]{:S(2)}, u32[]{:S(2)}) collective-permute-start(f32[2,32,1024]{2,1,0:T(8,128)S(1)} %collective-permute-done.8.refs_6_), channel_id=1, source_target_pairs={{0,1},{1,0},{2,3},{3,2},{4,5},{5,4},{6,7},{7,6},{8,9},{9,8},{10,11... | collective-permute-start | bytes 786440 | tf_op jit(solution)/shard_map/ppermute | solution.py:36
  30.7 6.0 %collective-permute-done.10.refs_8_ = f32[2,32,1024]{2,1,0:T(8,128)} collective-permute-done((f32[2,32,1024]{2,1,0:T(8,128)S(1)}, f32[2,32,1024]{2,1,0:T(8,128)}, u32[]{:S(2)}, u32[]{:S(2)}) %collective-permute-start.10) | collective-permute-done | bytes 262176 | tf_op jit(solution)/shard_map/ppermute | solution.py:32
  36.7 0.9 collective-permute-start.11
  37.5 1.9 %copy-done = f32[1,256,3,1024]{3,1,2,0:T(8,128)S(1)} copy-done((f32[1,256,3,1024]{3,1,2,0:T(8,128)S(1)}, f32[1,256,3,1024]{3,1,2,0:T(8,128)}, u32[]{:S(2)}) %copy-start) | copy-done | bytes 3145752
  39.4 0.7 copy-done.1
  40.1 0.9 prepare.1
  41.0 0.1 pad_add_fusion.coord
  41.1 0.0 collective-permute-done.9.refs_7_
  41.1 0.0 collective-permute-done.7.refs_5_
  41.1 0.0 collective-permute-done.11.refs_9_
  41.1 15.1 %build.1 = bf16[128,72,128]{2,1,0:T(8,128)(2,1)S(1)} custom-call(s32[3]{0:T(128)S(1)} %pad_add_fusion.coord, f32[4,32,1024]{2,1,0:T(8,128)S(1)} %pad_maximum_fusion.refs_0_, f32[4,32,1024]{2,1,0:T(8,128)S(1)} %collective-permute-done.3.refs_1_, f32[4,32,1024]{2,1,0:T(8,128)S(1)} %collective-permute-done.4.refs_2_, ...), custom_call_target="tpu_custom_call" | custom-call | tf_op jit(solution)/shard_map/build/pallas_call | solution.py:173
  56.1 38.2 %all_to_all.5.received = bf16[128,72,128]{2,1,0:T(8,128)(2,1)S(1)} all-to-all(bf16[128,72,128]{2,1,0:T(8,128)(2,1)S(1)} %build.1), channel_id=1, replica_groups=mesh['inlet'=4,'row'=32] {'inlet','row'}, dimensions={0} | all-to-all | bytes 4718592 | tf_op jit(solution)/shard_map/all_to_all | solution.py:278
  94.3 2.8 %settle.1 = bf16[3,384,1024]{2,1,0:T(8,128)(2,1)} custom-call(bf16[128,72,128]{2,1,0:T(8,128)(2,1)S(1)} %all_to_all.5.received), custom_call_target="tpu_custom_call" | custom-call | tf_op jit(solution)/shard_map/settle/pallas_call | solution.py:238
  (4 shorter events, 0.0 us)
Async XLA Ops:
  0.0 6.1 %collective-permute-start.2 = (f32[32,1024]{1,0:T(8,128)}, f32[32,1024]{1,0:T(8,128)S(1)}, u32[]{:S(2)}, u32[]{:S(2)}) collective-permute-start(f32[32,1024]{1,0:T(8,128)} %bitcast.14), channel_id=1, source_target_pairs={{0,16},{1,5},{2,18},{3,7},{4,20},{5,1},{6,22},{7,3},{8,24},{9,13},... | collective-permute-start | bytes 393224 | tf_op jit(solution)/shard_map/ppermute | solution.py:32
  3.6 4.6 %collective-permute-start.1 = (f32[32,1024]{1,0:T(8,128)}, f32[32,1024]{1,0:T(8,128)S(1)}, u32[]{:S(2)}, u32[]{:S(2)}) collective-permute-start(f32[32,1024]{1,0:T(8,128)} %bitcast.15), channel_id=1, source_target_pairs={{0,24},{1,7},{2,26},{3,1},{4,28},{5,3},{6,30},{7,5},{8,0},{9,15},{... | collective-permute-start | bytes 393224 | tf_op jit(solution)/shard_map/ppermute | solution.py:32
  4.4 5.2 %collective-permute-start = (f32[32,1024]{1,0:T(8,128)}, f32[32,1024]{1,0:T(8,128)S(1)}, u32[]{:S(2)}, u32[]{:S(2)}) collective-permute-start(f32[32,1024]{1,0:T(8,128)} %bitcast.16), channel_id=1, source_target_pairs={{0,8},{1,3},{2,10},{3,5},{4,12},{5,7},{6,14},{7,1},{8,16},{9,11},{... | collective-permute-start | bytes 393224 | tf_op jit(solution)/shard_map/ppermute | solution.py:32
  10.6 12.8 %collective-permute-start.6 = (f32[4,32,1024]{2,1,0:T(8,128)S(1)}, f32[4,32,1024]{2,1,0:T(8,128)S(1)}, u32[]{:S(2)}, u32[]{:S(2)}) collective-permute-start(f32[4,32,1024]{2,1,0:T(8,128)S(1)} %pad_maximum_fusion.refs_0_), channel_id=1, source_target_pairs={{0,6},{1,25},{2,0},{3,27},{4,2},{5,29},{6,4},{7,31},{8,14},{9,1},{... | collective-permute-start | bytes 1572872 | tf_op jit(solution)/shard_map/ppermute | solution.py:32
  14.4 12.3 %collective-permute-start.4 = (f32[4,32,1024]{2,1,0:T(8,128)S(1)}, f32[4,32,1024]{2,1,0:T(8,128)S(1)}, u32[]{:S(2)}, u32[]{:S(2)}) collective-permute-start(f32[4,32,1024]{2,1,0:T(8,128)S(1)} %pad_maximum_fusion.refs_0_), channel_id=1, source_target_pairs={{0,2},{1,9},{2,4},{3,11},{4,6},{5,13},{6,0},{7,15},{8,10},{9,17},{... | collective-permute-start | bytes 1572872 | tf_op jit(solution)/shard_map/ppermute | solution.py:32
  14.4 15.0 %collective-permute-start.3 = (f32[4,32,1024]{2,1,0:T(8,128)S(1)}, f32[4,32,1024]{2,1,0:T(8,128)S(1)}, u32[]{:S(2)}, u32[]{:S(2)}) collective-permute-start(f32[4,32,1024]{2,1,0:T(8,128)S(1)} %pad_maximum_fusion.refs_0_), channel_id=1, source_target_pairs={{0,1},{1,0},{2,3},{3,2},{4,5},{5,4},{6,7},{7,6},{8,9},{9,8},{10,11... | collective-permute-start | bytes 1572872 | tf_op jit(solution)/shard_map/ppermute | solution.py:36
  17.2 12.4 %collective-permute-start.8 = (f32[2,32,1024]{2,1,0:T(8,128)S(1)}, f32[2,32,1024]{2,1,0:T(8,128)S(1)}, u32[]{:S(2)}, u32[]{:S(2)}) collective-permute-start(f32[2,32,1024]{2,1,0:T(8,128)S(1)} %pad_maximum_fusion.1), channel_id=1, source_target_pairs={{0,4},{1,17},{2,6},{3,19},{4,0},{5,21},{6,2},{7,23},{8,12},{9,25},... | collective-permute-start | bytes 786440 | tf_op jit(solution)/shard_map/ppermute | solution.py:32
  23.4 17.7 %collective-permute-start.7 = (f32[4,32,1024]{2,1,0:T(8,128)S(1)}, f32[4,32,1024]{2,1,0:T(8,128)S(1)}, u32[]{:S(2)}, u32[]{:S(2)}) collective-permute-start(f32[4,32,1024]{2,1,0:T(8,128)S(1)} %collective-permute-done.6.refs_4_), channel_id=1, source_target_pairs={{0,1},{1,0},{2,3},{3,2},{4,5},{5,4},{6,7},{7,6},{8,9},{9,8},{10,11... | collective-permute-start | bytes 1572872 | tf_op jit(solution)/shard_map/ppermute | solution.py:36
  26.8 14.3 %collective-permute-start.5 = (f32[4,32,1024]{2,1,0:T(8,128)S(1)}, f32[4,32,1024]{2,1,0:T(8,128)S(1)}, u32[]{:S(2)}, u32[]{:S(2)}) collective-permute-start(f32[4,32,1024]{2,1,0:T(8,128)S(1)} %collective-permute-done.4.refs_2_), channel_id=1, source_target_pairs={{0,1},{1,0},{2,3},{3,2},{4,5},{5,4},{6,7},{7,6},{8,9},{9,8},{10,11... | collective-permute-start | bytes 1572872 | tf_op jit(solution)/shard_map/ppermute | solution.py:36
  29.5 7.2 %collective-permute-start.10 = (f32[2,32,1024]{2,1,0:T(8,128)S(1)}, f32[2,32,1024]{2,1,0:T(8,128)}, u32[]{:S(2)}, u32[]{:S(2)}) collective-permute-start(f32[2,32,1024]{2,1,0:T(8,128)S(1)} %slice.6), channel_id=1, source_target_pairs={{0,16},{1,5},{2,18},{3,7},{4,20},{5,1},{6,22},{7,3},{8,24},{9,13},... | collective-permute-start | bytes 786440 | tf_op jit(solution)/shard_map/ppermute | solution.py:32
  29.6 11.5 %collective-permute-start.9 = (f32[2,32,1024]{2,1,0:T(8,128)S(1)}, f32[2,32,1024]{2,1,0:T(8,128)}, u32[]{:S(2)}, u32[]{:S(2)}) collective-permute-start(f32[2,32,1024]{2,1,0:T(8,128)S(1)} %collective-permute-done.8.refs_6_), channel_id=1, source_target_pairs={{0,1},{1,0},{2,3},{3,2},{4,5},{5,4},{6,7},{7,6},{8,9},{9,8},{10,11... | collective-permute-start | bytes 786440 | tf_op jit(solution)/shard_map/ppermute | solution.py:36
  36.7 4.4 %collective-permute-start.11 = (f32[2,32,1024]{2,1,0:T(8,128)}, f32[2,32,1024]{2,1,0:T(8,128)}, u32[]{:S(2)}, u32[]{:S(2)}) collective-permute-start(f32[2,32,1024]{2,1,0:T(8,128)} %collective-permute-done.10.refs_8_), channel_id=1, source_target_pairs={{0,1},{1,0},{2,3},{3,2},{4,5},{5,4},{6,7},{7,6},{8,9},{9,8},{10,11... | collective-permute-start | bytes 786440 | tf_op jit(solution)/shard_map/ppermute | solution.py:36
  37.5 1.9 %copy-start = (f32[1,256,3,1024]{3,1,2,0:T(8,128)S(1)}, f32[1,256,3,1024]{3,1,2,0:T(8,128)}, u32[]{:S(2)}) copy-start(f32[1,256,3,1024]{3,1,2,0:T(8,128)} %param.4) | copy-start | bytes 9437188
  39.4 0.7 copy-start.1
where the time goes:
time: 97.3 us; the launch traced here: 97.1 us
  blocking collectives  38.2 us (39%)
  starting transfers between devices  18.8 us (19%)
  Pallas kernels  18.7 us (19%)
  waiting for transfers between devices  16.8 us (17%)
  local copies, waits for them, and re-layouts  2.59 us (3%)
  other arithmetic  1.95 us (2%)
    all_to_all x1, blocking collectives, steps(): lax.all_to_all(message, ('inlet', 'row'), split_axis=0, concat_axis=0, ti...  38.2 us
    ppermute x7, waiting for transfers between devices, turn(): return lax.ppermute(array, 'row', pairs)  16.8 us
    pallas_call x1, Pallas kernels, build(): pl.pallas_call(functools.partial(build_kernel, layout, rows), out_shape=j...  15.1 us
    ppermute x7, starting transfers between devices, turn(): return lax.ppermute(array, 'row', pairs)  9.9 us
    ppermute x5, starting transfers between devices, partner(): lax.ppermute(array, 'row', [(i, i ^ 1) for i in range(2 * SIDE * SIDE)])  8.9 us
    pallas_call x1, Pallas kernels, settle(): pl.pallas_call(functools.partial(settle_kernel, count), out_shape=jax.Sha...  2.83 us
    unnamed x4, local copies, waits for them, and re-layouts  2.57 us
  transfers between devices with their start and end apart: 12, of which 6 were waited for; matrix products, arithmetic and copies ran while one was open for 1% of the time, Pallas kernels for 1%

commit v1 on v0

v1 whole, which is shorter than its diff:
```python
import functools

import jax
import jax.numpy as jnp
from jax import lax
from jax.experimental import pallas as pl
from jax.experimental.pallas import tpu as pltpu
from jax.sharding import PartitionSpec as P


SIDE = 4
DEVICES = 128
CAP = 3
COMPS = 3
LANES = 128


def place(z, x, c):
    return (z * SIDE + x) * 2 + c


def turn(array, first, second, k):
    pairs = []
    for z in range(SIDE):
        for x in range(SIDE):
            for c in range(2):
                axis = (first, second)[c]
                tz = (z + k) % SIDE if axis == "z" else z
                tx = (x + k) % SIDE if axis == "x" else x
                pairs.append((place(z, x, c), place(tz, tx, c)))
    return lax.ppermute(array, "row", pairs)


def partner(array):
    return lax.ppermute(array, "row", [(i, i ^ 1) for i in range(2 * SIDE * SIDE)])


def split(value):
    high = value.astype(jnp.bfloat16)
    return high, (value - high.astype(jnp.float32)).astype(jnp.bfloat16)


def prepare_kernel(points, route, basis, high, low, picks_out, base, picks, sems, sem):
    copies = [
        pltpu.make_async_copy(basis.at[comp], base.at[comp], sems.at[comp]) for comp in range(COMPS)
    ]
    for copy in copies:
        copy.start()
    mine = lax.broadcasted_iota(jnp.int32, (DEVICES, points), 0) == route[...]
    before = lax.broadcasted_iota(jnp.int32, (points, points), 0) < lax.broadcasted_iota(
        jnp.int32, (points, points), 1
    )
    count = jnp.dot(
        jnp.where(mine, 1.0, 0.0).astype(jnp.bfloat16),
        jnp.where(before, 1.0, 0.0).astype(jnp.bfloat16),
        preferred_element_type=jnp.float32,
    )
    for r in range(CAP):
        picks[pl.ds(r * DEVICES, DEVICES), :] = jnp.where(
            mine & (count == float(r)), 1.0, 0.0
        ).astype(jnp.bfloat16)
    copy = pltpu.make_async_copy(picks, picks_out, sem)
    copy.start()
    for comp in range(COMPS):
        copies[comp].wait()
        high[pl.ds(comp * points, points), :], low[pl.ds(comp * points, points), :] = split(
            base[comp]
        )
    copy.wait()


def prepare(route, basis):
    comps, points, modes = basis.shape
    whole = pl.BlockSpec(memory_space=pltpu.VMEM)
    half = jax.ShapeDtypeStruct((comps * points, modes), jnp.bfloat16)
    return pl.pallas_call(
        functools.partial(prepare_kernel, points),
        out_shape=(half, half, jax.ShapeDtypeStruct((CAP * DEVICES, points), jnp.bfloat16)),
        in_specs=[whole, pl.BlockSpec(memory_space=pltpu.HBM)],
        out_specs=(whole, whole, pl.BlockSpec(memory_space=pltpu.HBM)),
        scratch_shapes=[
            pltpu.VMEM((comps, points, modes), jnp.float32),
            pltpu.VMEM((CAP * DEVICES, points), jnp.bfloat16),
            pltpu.SemaphoreType.DMA((comps,)),
            pltpu.SemaphoreType.DMA,
        ],
        compiler_params=pltpu.CompilerParams(vmem_limit_bytes=10 << 20),
        cost_estimate=pl.CostEstimate(flops=20_000_000, bytes_accessed=8 << 20, transcendentals=0),
        name="prepare",
    )(route, basis)


def product(points, coef, high, low, result):
    contract = functools.partial(
        lax.dot_general,
        dimension_numbers=(((1,), (1,)), ((), ())),
        preferred_element_type=jnp.float32,
    )
    top, rest = split(coef)
    for comp in range(COMPS):
        there = pl.ds(comp * points, points)
        value = contract(rest, high[there, :])
        value = value + contract(top, low[there, :])
        value = value + contract(top, high[there, :])
        value = value.astype(jnp.bfloat16)
        result[:, :, comp * points : (comp + 1) * points] = value.reshape(
            result.shape[:2] + (points,)
        )


def gathered(pieces):
    modes = pieces[0].shape[-1]
    return jnp.concatenate([piece[...].reshape(-1, modes) for piece in pieces], axis=0)


def expand_kernel(points, high, low, mine, mate, out, result, sem):
    product(points, gathered((mine, mate)), high, low, result)
    copy = pltpu.make_async_copy(result, out, sem)
    copy.start()
    copy.wait()


def expand(mine, mate, high, low, points):
    rows = mine.shape[1]
    shape = (8, rows, COMPS * points)
    return pl.pallas_call(
        functools.partial(expand_kernel, points),
        out_shape=jax.ShapeDtypeStruct(shape, jnp.bfloat16),
        in_specs=[pl.BlockSpec(memory_space=pltpu.VMEM)] * 4,
        out_specs=pl.BlockSpec(memory_space=pltpu.HBM),
        scratch_shapes=[pltpu.VMEM(shape, jnp.bfloat16), pltpu.SemaphoreType.DMA],
        compiler_params=pltpu.CompilerParams(vmem_limit_bytes=10 << 20),
        cost_estimate=pl.CostEstimate(
            flops=1_200_000_000, bytes_accessed=1 << 20, transcendentals=0
        ),
        name="expand",
    )(high, low, mine, mate)


def build_kernel(points, rows, *refs):
    lines, pieces = refs[:3], refs[3:7]
    high, low, picks_in, message = refs[7:11]
    table, picks, chunk, spread, in_sems = refs[11:]
    row = lax.axis_index("row")
    z = row // (2 * SIDE)
    x = lax.rem(row // 2, SIDE)
    c = lax.rem(row, 2)
    copies = [
        pltpu.make_async_copy(line, table.at[k], in_sems.at[i])
        for i, (line, k) in enumerate(zip(lines, (0, 1, 3)))
    ]
    copies.append(pltpu.make_async_copy(picks_in, picks, in_sems.at[3]))
    for copy in copies:
        copy.start()
    product(points, gathered(pieces), high, low, table.at[2])
    for copy in copies:
        copy.wait()

    width = 8 * rows
    blocks = width // LANES

    def step(i, _):
        dz = lax.rem(z - i + SIDE, SIDE)
        for column in range(SIDE):
            dx = lax.rem(x - column + SIDE, SIDE)
            for core in range(2):
                k, inner = (dx, dz) if core == 0 else (dz, dx)
                side = jnp.where(c == core, 0, SIDE)
                chunk[pl.ds((column * 2 + core) * rows, rows), :] = table[k, side + inner]
        for comp in range(COMPS):
            moved = lax.dot_general(
                picks[...],
                chunk[:, comp * points : (comp + 1) * points],
                (((1,), (1,)), ((), ())),
                preferred_element_type=jnp.float32,
            )
            for r in range(CAP):
                for half in range(blocks):
                    spread[r * COMPS + comp, pl.ds(i * blocks + half, DEVICES, stride=8), :] = (
                        moved[
                            r * DEVICES : (r + 1) * DEVICES, half * LANES : (half + 1) * LANES
                        ]
                    )
        return 0

    lax.fori_loop(0, SIDE, step, 0)
    part = DEVICES // 8

    def pack(i, _):
        for row in range(CAP * COMPS):
            message[pl.ds(i * part, part), pl.ds(row * 8, 8), :] = (
                spread[row, pl.ds(pl.multiple_of(i * part * 8, part * 8), part * 8), :]
                .reshape(part, 8, LANES)
                .astype(jnp.bfloat16)
            )
        return 0

    lax.fori_loop(0, 8, pack, 0)


def build(lines, pieces, high, low, picks):
    rows, wide = lines[0].shape[1:]
    points = picks.shape[1]
    remote = pl.BlockSpec(memory_space=pltpu.HBM)
    whole = pl.BlockSpec(memory_space=pltpu.VMEM)
    sent = (DEVICES, CAP * COMPS * 8, LANES)
    return pl.pallas_call(
        functools.partial(build_kernel, points, rows),
        out_shape=jax.ShapeDtypeStruct(sent, jnp.bfloat16),
        in_specs=[remote] * 3 + [whole] * 6 + [remote],
        out_specs=whole,
        scratch_shapes=[
            pltpu.VMEM((SIDE, 8, rows, wide), jnp.bfloat16),
            pltpu.VMEM(picks.shape, jnp.bfloat16),
            pltpu.VMEM((8 * rows, wide), jnp.bfloat16),
            pltpu.VMEM((CAP * COMPS, DEVICES * 8, LANES), jnp.float32),
            pltpu.SemaphoreType.DMA((4,)),
        ],
        compiler_params=pltpu.CompilerParams(vmem_limit_bytes=20 << 20),
        name="build",
    )(*lines, *pieces, high, low, picks)


def settle_kernel(count, received, out, wide, narrow, ready, out_sems):
    parts = DEVICES // count

    def lines(i):
        return pl.ds(pl.multiple_of(i * count * CAP, count * CAP), count * CAP)

    def leave(i):
        return pltpu.make_async_copy(ready.at[:, lines(i)], out.at[:, lines(i)], out_sems.at[i])

    def step(i, _):
        wide[...] = (
            received[pl.ds(i * count, count)].reshape(count * 72, LANES).astype(jnp.float32)
        )
        for comp in range(COMPS):
            for j in range(8):
                for r in range(CAP):
                    narrow[comp * 8 + j, pl.ds(r, count, stride=CAP), :] = wide[
                        pl.ds((r * COMPS + comp) * 8 + j, count, stride=72), :
                    ]
        for comp in range(COMPS):
            for j in range(8):
                ready[comp, lines(i), j * LANES : (j + 1) * LANES] = narrow[comp * 8 + j].astype(
                    jnp.bfloat16
                )
        leave(i).start()
        return 0

    lax.fori_loop(0, parts, step, 0)
    for i in range(parts):
        leave(i).wait()


def settle(received):
    count = 16
    shape = (COMPS, DEVICES * CAP, 8 * LANES)
    return pl.pallas_call(
        functools.partial(settle_kernel, count),
        out_shape=jax.ShapeDtypeStruct(shape, jnp.bfloat16),
        in_specs=[pl.BlockSpec(memory_space=pltpu.VMEM)],
        out_specs=pl.BlockSpec(memory_space=pl.ANY),
        scratch_shapes=[
            pltpu.VMEM((count * 72, LANES), jnp.float32),
            pltpu.VMEM((COMPS * 8, count * CAP, LANES), jnp.float32),
            pltpu.VMEM(shape, jnp.bfloat16),
            pltpu.SemaphoreType.DMA((DEVICES // count,)),
        ],
        compiler_params=pltpu.CompilerParams(vmem_limit_bytes=9 << 20),
        name="settle",
    )(received)


def steps(coeffs, basis, route):
    points = basis.shape[1]
    high, low, picks = prepare(route.reshape(1, -1), jnp.transpose(basis[0], (1, 0, 2)))
    own = coeffs[0]
    near = [own]
    for k in range(1, SIDE):
        near.append(turn(own, "z", "x", k))
    line = jnp.stack(near)
    mate = partner(line)

    def far(array, first, second, k):
        moved = turn(array, first, second, k)
        return moved, partner(moved)

    lines = []
    lines.append(expand(line, mate, high, low, points))
    for k in (1, 3):
        moved, swapped = far(line, "x", "z", k)
        lines.append(expand(moved, swapped, high, low, points))
    a, a_swapped = far(line[:2], "x", "z", 2)
    b, b_swapped = far(mate[2:], "z", "x", 2)
    message = build(lines, (a, b_swapped, a_swapped, b), high, low, picks)
    received = lax.all_to_all(message, ("inlet", "row"), split_axis=0, concat_axis=0, tiled=True)
    return jnp.transpose(settle(received), (1, 0, 2))


def solution(mesh):
    in_specs = (P("inlet", "row", None), P("inlet", "row", None, None), P(("inlet", "row"), None))
    out_specs = P(("inlet", "row"), None, None)
    return jax.shard_map(steps, mesh=mesh, in_specs=in_specs, out_specs=out_specs, check_vma=False)
```

time: 97.3 us -> 88.9 us (0.914)
  Pallas kernels: 18.7 us -> 12.6 us
  waiting for transfers between devices: 16.8 us -> 11.5 us
  starting transfers between devices: 18.8 us -> 20.5 us
  blocking collectives: 38.2 us -> 39.6 us
    pallas_call x1 -> x4, Pallas kernels: 15.1 us -> 9.17 us  [the longest x3 4.89 us: expand(): pl.pallas_call(functools.partial(expand_kernel, points), out_shape=jax.Sh...]
    ppermute x7, waiting for transfers between devices: 16.8 us -> 11.5 us  [turn(): return lax.ppermute(array, 'row', pairs)]
    ppermute x7, starting transfers between devices: 9.9 us -> 11.5 us  [turn(): return lax.ppermute(array, 'row', pairs)]
    all_to_all x1, blocking collectives: 38.2 us -> 39.6 us  [steps(): lax.all_to_all(message, ('inlet', 'row'), split_axis=0, concat_axis=0, ti...]
  transfers between devices with their start and end apart: 12 -> 12, of which waited for: 6 -> 7; matrix products, arithmetic and copies ran while one was open for 1% -> 1% of each run, Pallas kernels for 1% -> 7%
where the time goes in v1:
time: 88.9 us; the launch traced here: 88.7 us
  blocking collectives  39.6 us (45%)
  starting transfers between devices  20.5 us (23%)
  Pallas kernels  12.6 us (14%)
  waiting for transfers between devices  11.5 us (13%)
  local copies, waits for them, and re-layouts  2.58 us (3%)
  other arithmetic  1.87 us (2%)
    all_to_all x1, blocking collectives, steps(): lax.all_to_all(message, ('inlet', 'row'), split_axis=0, concat_axis=0, ti...  39.6 us
    ppermute x7, starting transfers between devices, turn(): return lax.ppermute(array, 'row', pairs)  11.5 us
    ppermute x7, waiting for transfers between devices, turn(): return lax.ppermute(array, 'row', pairs)  11.5 us
    ppermute x5, starting transfers between devices, partner(): lax.ppermute(array, 'row', [(i, i ^ 1) for i in range(2 * SIDE * SIDE)])  8.96 us
    pallas_call x3, Pallas kernels, expand(): pl.pallas_call(functools.partial(expand_kernel, points), out_shape=jax.Sh...  4.89 us
    pallas_call x1, Pallas kernels, build(): pl.pallas_call(functools.partial(build_kernel, points, rows), out_shape=j...  4.28 us
    unnamed x4, local copies, waits for them, and re-layouts  2.56 us
    pallas_call x1, Pallas kernels, settle(): pl.pallas_call(functools.partial(settle_kernel, count), out_shape=jax.Sha...  2.28 us
  transfers between devices with their start and end apart: 12, of which 7 were waited for; matrix products, arithmetic and copies ran while one was open for 1% of the time, Pallas kernels for 7%

profile of v1, /device:TPU:1, one launch (start us, length us, event | category | flops | bytes accessed | tf_op | source)
XLA Modules:
  0.0 88.7 jit_solution(3344101619709507542)
XLA Ops:
  0.0 2.0 %collective-permute-start = (f32[32,1024]{1,0:T(8,128)}, f32[32,1024]{1,0:T(8,128)S(1)}, u32[]{:S(2)}, u32[]{:S(2)}) collective-permute-start(f32[32,1024]{1,0:T(8,128)} %bitcast.11), channel_id=1, source_target_pairs={{0,8},{1,3},{2,10},{3,5},{4,12},{5,7},{6,14},{7,1},{8,16},{9,11},{... | collective-permute-start | bytes 393224 | tf_op jit(solution)/shard_map/ppermute | solution.py:31
  2.0 2.5 %collective-permute-start.1 = (f32[32,1024]{1,0:T(8,128)}, f32[32,1024]{1,0:T(8,128)S(1)}, u32[]{:S(2)}, u32[]{:S(2)}) collective-permute-start(f32[32,1024]{1,0:T(8,128)} %bitcast.12), channel_id=1, source_target_pairs={{0,16},{1,5},{2,18},{3,7},{4,20},{5,1},{6,22},{7,3},{8,24},{9,13},... | collective-permute-start | bytes 393224 | tf_op jit(solution)/shard_map/ppermute | solution.py:31
  4.5 1.2 %collective-permute-start.2 = (f32[32,1024]{1,0:T(8,128)}, f32[32,1024]{1,0:T(8,128)S(1)}, u32[]{:S(2)}, u32[]{:S(2)}) collective-permute-start(f32[32,1024]{1,0:T(8,128)} %bitcast.13), channel_id=1, source_target_pairs={{0,24},{1,7},{2,26},{3,1},{4,28},{5,3},{6,30},{7,5},{8,0},{9,15},{... | collective-permute-start | bytes 393224 | tf_op jit(solution)/shard_map/ppermute | solution.py:31
  5.6 0.2 collective-permute-done
  5.9 2.6 %collective-permute-done.1 = f32[32,1024]{1,0:T(8,128)S(1)} collective-permute-done((f32[32,1024]{1,0:T(8,128)}, f32[32,1024]{1,0:T(8,128)S(1)}, u32[]{:S(2)}, u32[]{:S(2)}) %collective-permute-start.1) | collective-permute-done | bytes 131104 | tf_op jit(solution)/shard_map/ppermute | solution.py:31
  8.4 0.1 collective-permute-done.2
  8.5 0.9 %pad_maximum_fusion.mine = f32[4,32,1024]{2,1,0:T(8,128)S(1)} fusion(f32[1,32,1024]{2,1,0:T(8,128)S(1)} %bitcast.17, f32[1,32,1024]{2,1,0:T(8,128)S(1)} %bitcast.16, f32[1,32,1024]{2,1,0:T(8,128)S(1)} %bitcast.14, f32[1,32,1024]{2,1,0:T(8,128)} %param.3), kind=kLoop, calls=%fused_computation | loop fusion | flops 393216 | bytes 1048576 | tf_op jit(solution)/shard_map/stack | solution.py:282
  9.5 4.1 %collective-permute-start.6 = (f32[4,32,1024]{2,1,0:T(8,128)S(1)}, f32[4,32,1024]{2,1,0:T(8,128)S(1)}, u32[]{:S(2)}, u32[]{:S(2)}) collective-permute-start(f32[4,32,1024]{2,1,0:T(8,128)S(1)} %pad_maximum_fusion.mine), channel_id=1, source_target_pairs={{0,6},{1,25},{2,0},{3,27},{4,2},{5,29},{6,4},{7,31},{8,14},{9,1},{... | collective-permute-start | bytes 1572872 | tf_op jit(solution)/shard_map/ppermute | solution.py:31
  13.6 2.4 %collective-permute-start.3 = (f32[4,32,1024]{2,1,0:T(8,128)S(1)}, f32[4,32,1024]{2,1,0:T(8,128)S(1)}, u32[]{:S(2)}, u32[]{:S(2)}) collective-permute-start(f32[4,32,1024]{2,1,0:T(8,128)S(1)} %pad_maximum_fusion.mine), channel_id=1, source_target_pairs={{0,1},{1,0},{2,3},{3,2},{4,5},{5,4},{6,7},{7,6},{8,9},{9,8},{10,11... | collective-permute-start | bytes 1572872 | tf_op jit(solution)/shard_map/ppermute | solution.py:35
  16.0 3.8 %collective-permute-done.6.mine = f32[4,32,1024]{2,1,0:T(8,128)S(1)} collective-permute-done((f32[4,32,1024]{2,1,0:T(8,128)S(1)}, f32[4,32,1024]{2,1,0:T(8,128)S(1)}, u32[]{:S(2)}, u32[]{:S(2)}) %collective-permute-start.6) | collective-permute-done | bytes 524320 | tf_op jit(solution)/shard_map/ppermute | solution.py:31
  19.7 2.9 %collective-permute-start.7 = (f32[4,32,1024]{2,1,0:T(8,128)S(1)}, f32[4,32,1024]{2,1,0:T(8,128)S(1)}, u32[]{:S(2)}, u32[]{:S(2)}) collective-permute-start(f32[4,32,1024]{2,1,0:T(8,128)S(1)} %collective-permute-done.6.mine), channel_id=1, source_target_pairs={{0,1},{1,0},{2,3},{3,2},{4,5},{5,4},{6,7},{7,6},{8,9},{9,8},{10,11... | collective-permute-start | bytes 1572872 | tf_op jit(solution)/shard_map/ppermute | solution.py:35
  22.7 0.5 collective-permute-done.4.mine
  23.1 3.2 %collective-permute-start.5 = (f32[4,32,1024]{2,1,0:T(8,128)S(1)}, f32[4,32,1024]{2,1,0:T(8,128)S(1)}, u32[]{:S(2)}, u32[]{:S(2)}) collective-permute-start(f32[4,32,1024]{2,1,0:T(8,128)S(1)} %collective-permute-done.4.mine), channel_id=1, source_target_pairs={{0,1},{1,0},{2,3},{3,2},{4,5},{5,4},{6,7},{7,6},{8,9},{9,8},{10,11... | collective-permute-start | bytes 1572872 | tf_op jit(solution)/shard_map/ppermute | solution.py:35
  26.3 0.9 %pad_maximum_fusion.1 = f32[2,32,1024]{2,1,0:T(8,128)S(1)} fusion(f32[1,32,1024]{2,1,0:T(8,128)S(1)} %bitcast.15, f32[1,32,1024]{2,1,0:T(8,128)} %param.3), kind=kLoop, calls=%fused_computation.1 | loop fusion | flops 65536 | bytes 524288 | tf_op jit(solution)/shard_map/stack | solution.py:282
  27.3 1.7 %collective-permute-start.8 = (f32[2,32,1024]{2,1,0:T(8,128)S(1)}, f32[2,32,1024]{2,1,0:T(8,128)S(1)}, u32[]{:S(2)}, u32[]{:S(2)}) collective-permute-start(f32[2,32,1024]{2,1,0:T(8,128)S(1)} %pad_maximum_fusion.1), channel_id=1, source_target_pairs={{0,4},{1,17},{2,6},{3,19},{4,0},{5,21},{6,2},{7,23},{8,12},{9,25},... | collective-permute-start | bytes 786440 | tf_op jit(solution)/shard_map/ppermute | solution.py:31
  29.0 0.0 collective-permute-done.3.mate
  29.0 0.1 collective-permute-start.9
  29.1 0.0 copy-start
  29.1 1.9 %copy-done = f32[1,256,3,1024]{3,1,2,0:T(8,128)S(1)} copy-done((f32[1,256,3,1024]{3,1,2,0:T(8,128)S(1)}, f32[1,256,3,1024]{3,1,2,0:T(8,128)}, u32[]{:S(2)}) %copy-start) | copy-done | bytes 3145752
  31.0 0.7 copy-done.1
  31.7 1.1 %prepare.1 = (bf16[768,1024]{1,0:T(8,128)(2,1)S(1)}, bf16[768,1024]{1,0:T(8,128)(2,1)S(1)}, bf16[384,256]{1,0:T(8,128)(2,1)S(1)}) custom-call(s32[1,256]{1,0:T(1,128)S(1)} %bitcast.10, f32[3,256,1024]{2,1,0:T(8,128)S(1)} %bitcast.9), custom_call_target="tpu_custom_call" | custom-call | flops 20000000 | bytes 8388608 | tf_op jit(solution)/shard_map/prepare/pallas_call | solution.py:76
  32.8 3.8 %collective-permute-done.8.refs_3_ = f32[2,32,1024]{2,1,0:T(8,128)S(1)} collective-permute-done((f32[2,32,1024]{2,1,0:T(8,128)S(1)}, f32[2,32,1024]{2,1,0:T(8,128)S(1)}, u32[]{:S(2)}, u32[]{:S(2)}) %collective-permute-start.8) | collective-permute-done | bytes 262176 | tf_op jit(solution)/shard_map/ppermute | solution.py:31
  36.6 0.2 collective-permute-start.11
  36.8 0.6 collective-permute-done.9.refs_6_
  37.3 0.2 collective-permute-start.10
  37.6 1.6 %expand.3.refs_0_ = bf16[8,32,768]{2,1,0:T(8,128)(2,1)S(1)} custom-call(bf16[768,1024]{1,0:T(8,128)(2,1)S(1)} %get-tuple-element.8.high.refs_7_, bf16[768,1024]{1,0:T(8,128)(2,1)S(1)} %get-tuple-element.9.low.refs_8_, f32[4,32,1024]{2,1,0:T(8,128)S(1)} %pad_maximum_fusion.mine, f32[4,32,1024]{2,1,0:T(8,128)S(1)} %collective-permute-done.3.mate), custom_call_target="tpu_custom_call" | custom-call | flops 1200000000 | bytes 1048576 | tf_op jit(solution)/shard_map/expand/pallas_call | solution.py:126
  39.2 0.0 collective-permute-done.7.mate
  39.2 1.6 %expand.5.refs_2_ = bf16[8,32,768]{2,1,0:T(8,128)(2,1)S(1)} custom-call(bf16[768,1024]{1,0:T(8,128)(2,1)S(1)} %get-tuple-element.8.high.refs_7_, bf16[768,1024]{1,0:T(8,128)(2,1)S(1)} %get-tuple-element.9.low.refs_8_, f32[4,32,1024]{2,1,0:T(8,128)S(1)} %collective-permute-done.6.mine, f32[4,32,1024]{2,1,0:T(8,128)S(1)} %collective-permute-done.7.mate), custom_call_target="tpu_custom_call" | custom-call | flops 1200000000 | bytes 1048576 | tf_op jit(solution)/shard_map/expand/pallas_call | solution.py:126
  40.9 1.6 %expand.4.refs_1_ = bf16[8,32,768]{2,1,0:T(8,128)(2,1)S(1)} custom-call(bf16[768,1024]{1,0:T(8,128)(2,1)S(1)} %get-tuple-element.8.high.refs_7_, bf16[768,1024]{1,0:T(8,128)(2,1)S(1)} %get-tuple-element.9.low.refs_8_, f32[4,32,1024]{2,1,0:T(8,128)S(1)} %collective-permute-done.4.mine, f32[4,32,1024]{2,1,0:T(8,128)S(1)} %collective-permute-done.5.mate), custom_call_target="tpu_custom_call" | custom-call | flops 1200000000 | bytes 1048576 | tf_op jit(solution)/shard_map/expand/pallas_call | solution.py:126
  42.5 4.3 %build.1 = bf16[128,72,128]{2,1,0:T(8,128)(2,1)S(1)} custom-call(bf16[8,32,768]{2,1,0:T(8,128)(2,1)S(1)} %expand.3.refs_0_, bf16[8,32,768]{2,1,0:T(8,128)(2,1)S(1)} %expand.4.refs_1_, bf16[8,32,768]{2,1,0:T(8,128)(2,1)S(1)} %expand.5.refs_2_, f32[2,32,1024]{2,1,0:T(8,128)S(1)} %collective-permute-done.8.refs_3_, ...), custom_call_target="tpu_custom_call" | custom-call | tf_op jit(solution)/shard_map/build/pallas_call | solution.py:207
  46.8 39.6 %all_to_all.5.received = bf16[128,72,128]{2,1,0:T(8,128)(2,1)S(1)} all-to-all(bf16[128,72,128]{2,1,0:T(8,128)(2,1)S(1)} %build.1), channel_id=1, replica_groups=mesh['inlet'=4,'row'=32] {'inlet','row'}, dimensions={0} | all-to-all | bytes 4718592 | tf_op jit(solution)/shard_map/all_to_all | solution.py:297
  86.4 2.3 %settle.1 = bf16[3,384,1024]{2,1,0:T(8,128)(2,1)} custom-call(bf16[128,72,128]{2,1,0:T(8,128)(2,1)S(1)} %all_to_all.5.received), custom_call_target="tpu_custom_call" | custom-call | tf_op jit(solution)/shard_map/settle/pallas_call | solution.py:259
  (6 shorter events, 0.0 us)
Async XLA Ops:
  0.0 5.9 %collective-permute-start = (f32[32,1024]{1,0:T(8,128)}, f32[32,1024]{1,0:T(8,128)S(1)}, u32[]{:S(2)}, u32[]{:S(2)}) collective-permute-start(f32[32,1024]{1,0:T(8,128)} %bitcast.11), channel_id=1, source_target_pairs={{0,8},{1,3},{2,10},{3,5},{4,12},{5,7},{6,14},{7,1},{8,16},{9,11},{... | collective-permute-start | bytes 393224 | tf_op jit(solution)/shard_map/ppermute | solution.py:31
  2.0 6.4 %collective-permute-start.1 = (f32[32,1024]{1,0:T(8,128)}, f32[32,1024]{1,0:T(8,128)S(1)}, u32[]{:S(2)}, u32[]{:S(2)}) collective-permute-start(f32[32,1024]{1,0:T(8,128)} %bitcast.12), channel_id=1, source_target_pairs={{0,16},{1,5},{2,18},{3,7},{4,20},{5,1},{6,22},{7,3},{8,24},{9,13},... | collective-permute-start | bytes 393224 | tf_op jit(solution)/shard_map/ppermute | solution.py:31
  4.5 4.0 %collective-permute-start.2 = (f32[32,1024]{1,0:T(8,128)}, f32[32,1024]{1,0:T(8,128)S(1)}, u32[]{:S(2)}, u32[]{:S(2)}) collective-permute-start(f32[32,1024]{1,0:T(8,128)} %bitcast.13), channel_id=1, source_target_pairs={{0,24},{1,7},{2,26},{3,1},{4,28},{5,3},{6,30},{7,5},{8,0},{9,15},{... | collective-permute-start | bytes 393224 | tf_op jit(solution)/shard_map/ppermute | solution.py:31
  9.5 10.2 %collective-permute-start.6 = (f32[4,32,1024]{2,1,0:T(8,128)S(1)}, f32[4,32,1024]{2,1,0:T(8,128)S(1)}, u32[]{:S(2)}, u32[]{:S(2)}) collective-permute-start(f32[4,32,1024]{2,1,0:T(8,128)S(1)} %pad_maximum_fusion.mine), channel_id=1, source_target_pairs={{0,6},{1,25},{2,0},{3,27},{4,2},{5,29},{6,4},{7,31},{8,14},{9,1},{... | collective-permute-start | bytes 1572872 | tf_op jit(solution)/shard_map/ppermute | solution.py:31
  13.6 9.5 %collective-permute-start.4 = (f32[4,32,1024]{2,1,0:T(8,128)S(1)}, f32[4,32,1024]{2,1,0:T(8,128)S(1)}, u32[]{:S(2)}, u32[]{:S(2)}) collective-permute-start(f32[4,32,1024]{2,1,0:T(8,128)S(1)} %pad_maximum_fusion.mine), channel_id=1, source_target_pairs={{0,2},{1,9},{2,4},{3,11},{4,6},{5,13},{6,0},{7,15},{8,10},{9,17},{... | collective-permute-start | bytes 1572872 | tf_op jit(solution)/shard_map/ppermute | solution.py:31
  13.6 15.4 %collective-permute-start.3 = (f32[4,32,1024]{2,1,0:T(8,128)S(1)}, f32[4,32,1024]{2,1,0:T(8,128)S(1)}, u32[]{:S(2)}, u32[]{:S(2)}) collective-permute-start(f32[4,32,1024]{2,1,0:T(8,128)S(1)} %pad_maximum_fusion.mine), channel_id=1, source_target_pairs={{0,1},{1,0},{2,3},{3,2},{4,5},{5,4},{6,7},{7,6},{8,9},{9,8},{10,11... | collective-permute-start | bytes 1572872 | tf_op jit(solution)/shard_map/ppermute | solution.py:35
  19.7 19.5 %collective-permute-start.7 = (f32[4,32,1024]{2,1,0:T(8,128)S(1)}, f32[4,32,1024]{2,1,0:T(8,128)S(1)}, u32[]{:S(2)}, u32[]{:S(2)}) collective-permute-start(f32[4,32,1024]{2,1,0:T(8,128)S(1)} %collective-permute-done.6.mine), channel_id=1, source_target_pairs={{0,1},{1,0},{2,3},{3,2},{4,5},{5,4},{6,7},{7,6},{8,9},{9,8},{10,11... | collective-permute-start | bytes 1572872 | tf_op jit(solution)/shard_map/ppermute | solution.py:35
  23.1 17.7 %collective-permute-start.5 = (f32[4,32,1024]{2,1,0:T(8,128)S(1)}, f32[4,32,1024]{2,1,0:T(8,128)S(1)}, u32[]{:S(2)}, u32[]{:S(2)}) collective-permute-start(f32[4,32,1024]{2,1,0:T(8,128)S(1)} %collective-permute-done.4.mine), channel_id=1, source_target_pairs={{0,1},{1,0},{2,3},{3,2},{4,5},{5,4},{6,7},{7,6},{8,9},{9,8},{10,11... | collective-permute-start | bytes 1572872 | tf_op jit(solution)/shard_map/ppermute | solution.py:35
  27.3 9.3 %collective-permute-start.8 = (f32[2,32,1024]{2,1,0:T(8,128)S(1)}, f32[2,32,1024]{2,1,0:T(8,128)S(1)}, u32[]{:S(2)}, u32[]{:S(2)}) collective-permute-start(f32[2,32,1024]{2,1,0:T(8,128)S(1)} %pad_maximum_fusion.1), channel_id=1, source_target_pairs={{0,4},{1,17},{2,6},{3,19},{4,0},{5,21},{6,2},{7,23},{8,12},{9,25},... | collective-permute-start | bytes 786440 | tf_op jit(solution)/shard_map/ppermute | solution.py:31
  29.0 8.4 %collective-permute-start.9 = (f32[2,32,1024]{2,1,0:T(8,128)S(1)}, f32[2,32,1024]{2,1,0:T(8,128)S(1)}, u32[]{:S(2)}, u32[]{:S(2)}) collective-permute-start(f32[2,32,1024]{2,1,0:T(8,128)S(1)} %slice.6), channel_id=1, source_target_pairs={{0,16},{1,5},{2,18},{3,7},{4,20},{5,1},{6,22},{7,3},{8,24},{9,13},... | collective-permute-start | bytes 786440 | tf_op jit(solution)/shard_map/ppermute | solution.py:31
  29.1 1.9 %copy-start = (f32[1,256,3,1024]{3,1,2,0:T(8,128)S(1)}, f32[1,256,3,1024]{3,1,2,0:T(8,128)}, u32[]{:S(2)}) copy-start(f32[1,256,3,1024]{3,1,2,0:T(8,128)} %param.4) | copy-start | bytes 9437188
  31.0 0.7 copy-start.1
  36.6 5.9 %collective-permute-start.11 = (f32[2,32,1024]{2,1,0:T(8,128)S(1)}, f32[2,32,1024]{2,1,0:T(8,128)S(1)}, u32[]{:S(2)}, u32[]{:S(2)}) collective-permute-start(f32[2,32,1024]{2,1,0:T(8,128)S(1)} %collective-permute-done.8.refs_3_), channel_id=1, source_target_pairs={{0,1},{1,0},{2,3},{3,2},{4,5},{5,4},{6,7},{7,6},{8,9},{9,8},{10,11... | collective-permute-start | bytes 786440 | tf_op jit(solution)/shard_map/ppermute | solution.py:35
  37.3 5.2 %collective-permute-start.10 = (f32[2,32,1024]{2,1,0:T(8,128)S(1)}, f32[2,32,1024]{2,1,0:T(8,128)S(1)}, u32[]{:S(2)}, u32[]{:S(2)}) collective-permute-start(f32[2,32,1024]{2,1,0:T(8,128)S(1)} %collective-permute-done.9.refs_6_), channel_id=1, source_target_pairs={{0,1},{1,0},{2,3},{3,2},{4,5},{5,4},{6,7},{7,6},{8,9},{9,8},{10,11... | collective-permute-start | bytes 786440 | tf_op jit(solution)/shard_map/ppermute | solution.py:35

commit v2 on v1

--- a/solution.py
+++ b/solution.py
@@ -5,6 +5,7 @@
 from jax import lax
 from jax.experimental import pallas as pl
 from jax.experimental.pallas import tpu as pltpu
+from jax.sharding import Mesh
 from jax.sharding import PartitionSpec as P
 
 
@@ -17,6 +18,15 @@
 
 def place(z, x, c):
     return (z * SIDE + x) * 2 + c
+
+
+def position(y, z, x, c):
+    return ((c * SIDE + z) * SIDE + y) * SIDE + x
+
+
+def device_at(slot):
+    y, z, x, c = (slot >> 2) & 3, (slot >> 4) & 3, slot & 3, slot >> 6
+    return ((y * SIDE + z) * SIDE + x) * 2 + c
 
 
 def turn(array, first, second, k):
@@ -28,11 +38,11 @@
                 tz = (z + k) % SIDE if axis == "z" else z
                 tx = (x + k) % SIDE if axis == "x" else x
                 pairs.append((place(z, x, c), place(tz, tx, c)))
-    return lax.ppermute(array, "row", pairs)
+    return lax.ppermute(array, ("z", "x", "c"), pairs)
 
 
 def partner(array):
-    return lax.ppermute(array, "row", [(i, i ^ 1) for i in range(2 * SIDE * SIDE)])
+    return lax.ppermute(array, ("z", "x", "c"), [(i, i ^ 1) for i in range(2 * SIDE * SIDE)])
 
 
 def split(value):
@@ -46,7 +56,7 @@
     ]
     for copy in copies:
         copy.start()
-    mine = lax.broadcasted_iota(jnp.int32, (DEVICES, points), 0) == route[...]
+    mine = device_at(lax.broadcasted_iota(jnp.int32, (DEVICES, points), 0)) == route[...]
     before = lax.broadcasted_iota(jnp.int32, (points, points), 0) < lax.broadcasted_iota(
         jnp.int32, (points, points), 1
     )
@@ -84,7 +94,7 @@
             pltpu.SemaphoreType.DMA((comps,)),
             pltpu.SemaphoreType.DMA,
         ],
-        compiler_params=pltpu.CompilerParams(vmem_limit_bytes=10 << 20),
+        compiler_params=pltpu.CompilerParams(vmem_limit_bytes=52_000_000),
         cost_estimate=pl.CostEstimate(flops=20_000_000, bytes_accessed=8 << 20, transcendentals=0),
         name="prepare",
     )(route, basis)
@@ -141,10 +151,7 @@
     lines, pieces = refs[:3], refs[3:7]
     high, low, picks_in, message = refs[7:11]
     table, picks, chunk, spread, in_sems = refs[11:]
-    row = lax.axis_index("row")
-    z = row // (2 * SIDE)
-    x = lax.rem(row // 2, SIDE)
-    c = lax.rem(row, 2)
+    z, x, c = lax.axis_index("z"), lax.axis_index("x"), lax.axis_index("c")
     copies = [
         pltpu.make_async_copy(line, table.at[k], in_sems.at[i])
         for i, (line, k) in enumerate(zip(lines, (0, 1, 3)))
@@ -223,6 +230,7 @@
 
 def settle_kernel(count, received, out, wide, narrow, ready, out_sems):
     parts = DEVICES // count
+    planes = count // (2 * SIDE)
 
     def lines(i):
         return pl.ds(pl.multiple_of(i * count * CAP, count * CAP), count * CAP)
@@ -231,15 +239,27 @@
         return pltpu.make_async_copy(ready.at[:, lines(i)], out.at[:, lines(i)], out_sems.at[i])
 
     def step(i, _):
-        wide[...] = (
-            received[pl.ds(i * count, count)].reshape(count * 72, LANES).astype(jnp.float32)
-        )
+        for core in range(2):
+            for plane in range(planes):
+                y, z = (i * planes + plane) // SIDE, lax.rem(i * planes + plane, SIDE)
+                run = received[pl.ds(position(y, z, 0, core), SIDE)]
+                wide[pl.ds((core * planes + plane) * SIDE * 72, SIDE * 72), :] = run.reshape(
+                    SIDE * 72, LANES
+                ).astype(jnp.float32)
         for comp in range(COMPS):
             for j in range(8):
                 for r in range(CAP):
-                    narrow[comp * 8 + j, pl.ds(r, count, stride=CAP), :] = wide[
-                        pl.ds((r * COMPS + comp) * 8 + j, count, stride=72), :
-                    ]
+                    for core in range(2):
+                        narrow[
+                            comp * 8 + j, pl.ds(core * CAP + r, count // 2, stride=2 * CAP), :
+                        ] = wide[
+                            pl.ds(
+                                core * count // 2 * 72 + (r * COMPS + comp) * 8 + j,
+                                count // 2,
+                                stride=72,
+                            ),
+                            :,
+                        ]
         for comp in range(COMPS):
             for j in range(8):
                 ready[comp, lines(i), j * LANES : (j + 1) * LANES] = narrow[comp * 8 + j].astype(
@@ -279,7 +299,7 @@
     near = [own]
     for k in range(1, SIDE):
         near.append(turn(own, "z", "x", k))
-    line = jnp.stack(near)
+    line = lax.optimization_barrier(jnp.stack(near))
     mate = partner(line)
 
     def far(array, first, second, k):
@@ -294,11 +314,14 @@
     a, a_swapped = far(line[:2], "x", "z", 2)
     b, b_swapped = far(mate[2:], "z", "x", 2)
     message = build(lines, (a, b_swapped, a_swapped, b), high, low, picks)
-    received = lax.all_to_all(message, ("inlet", "row"), split_axis=0, concat_axis=0, tiled=True)
+    received = lax.all_to_all(message, ("c", "z", "y", "x"), split_axis=0, concat_axis=0, tiled=True)
     return jnp.transpose(settle(received), (1, 0, 2))
 
 
 def solution(mesh):
-    in_specs = (P("inlet", "row", None), P("inlet", "row", None, None), P(("inlet", "row"), None))
-    out_specs = P(("inlet", "row"), None, None)
-    return jax.shard_map(steps, mesh=mesh, in_specs=in_specs, out_specs=out_specs, check_vma=False)
+    fine = Mesh(mesh.devices.reshape(SIDE, SIDE, SIDE, 2), ("y", "z", "x", "c"))
+    row = ("z", "x", "c")
+    everyone = ("y",) + row
+    in_specs = (P("y", row, None), P("y", row, None, None), P(everyone, None))
+    out_specs = P(everyone, None, None)
+    return jax.shard_map(steps, mesh=fine, in_specs=in_specs, out_specs=out_specs, check_vma=False)

time: 88.9 us -> 86.1 us (0.969)
  blocking collectives: 39.6 us -> 37.7 us
  local copies, waits for them, and re-layouts: 2.58 us -> 0.71 us
  Pallas kernels: 12.6 us -> 13.6 us
  other arithmetic: 1.87 us -> 0.95 us
  waiting for transfers between devices: 11.5 us -> 12.4 us
    all_to_all x1, blocking collectives: 39.6 us -> 37.7 us  [steps(): lax.all_to_all(message, ('c', 'z', 'y', 'x'), split_axis=0, concat_axis=0...]
    unnamed x4 -> x2, local copies, waits for them, and re-layouts: 2.56 us -> 0.67 us
    ppermute x12, waiting for transfers between devices: 11.5 us -> 12.4 us  [the longest x7 12.4 us: turn(): return lax.ppermute(array, ('z', 'x', 'c'), pairs)]
    pallas_call x1, Pallas kernels: 1.12 us -> 2.05 us  [prepare(): pl.pallas_call(functools.partial(prepare_kernel, points), out_shape=(half...]
    another operation x2 -> x1, other arithmetic: 1.87 us -> 0.95 us  [steps(): line = lax.optimization_barrier(jnp.stack(near))]
  transfers between devices with their start and end apart: 12 -> 12, of which waited for: 7 -> 7; matrix products, arithmetic and copies ran while one was open for 1% -> 0% of each run, Pallas kernels for 7% -> 8%
where the time goes in v2:
time: 86.1 us; the launch traced here: 86 us
  blocking collectives  37.7 us (44%)
  starting transfers between devices  20.5 us (24%)
  Pallas kernels  13.6 us (16%)
  waiting for transfers between devices  12.4 us (14%)
  other arithmetic  0.95 us (1%)
    all_to_all x1, blocking collectives, steps(): lax.all_to_all(message, ('c', 'z', 'y', 'x'), split_axis=0, concat_axis=0...  37.7 us
    ppermute x7, waiting for transfers between devices, turn(): return lax.ppermute(array, ('z', 'x', 'c'), pairs)  12.4 us
    ppermute x7, starting transfers between devices, turn(): return lax.ppermute(array, ('z', 'x', 'c'), pairs)  11.5 us
    ppermute x5, starting transfers between devices, partner(): lax.ppermute(array, ('z', 'x', 'c'), [(i, i ^ 1) for i in range(2 * SIDE...  8.96 us
    pallas_call x3, Pallas kernels, expand(): pl.pallas_call(functools.partial(expand_kernel, points), out_shape=jax.Sh...  4.93 us
    pallas_call x1, Pallas kernels, build(): pl.pallas_call(functools.partial(build_kernel, points, rows), out_shape=j...  4.29 us
    pallas_call x1, Pallas kernels, settle(): pl.pallas_call(functools.partial(settle_kernel, count), out_shape=jax.Sha...  2.34 us
    pallas_call x1, Pallas kernels, prepare(): pl.pallas_call(functools.partial(prepare_kernel, points), out_shape=(half...  2.05 us
  transfers between devices with their start and end apart: 12, of which 7 were waited for; matrix products, arithmetic and copies ran while one was open for 0% of the time, Pallas kernels for 8%

profile of v2, /device:TPU:1, one launch (start us, length us, event | category | flops | bytes accessed | tf_op | source)
XLA Modules:
  0.0 86.0 jit_solution(3481118023611795225)
XLA Ops:
  0.0 2.0 %collective-permute-start = (f32[32,1024]{1,0:T(8,128)}, f32[32,1024]{1,0:T(8,128)S(1)}, u32[]{:S(2)}, u32[]{:S(2)}) collective-permute-start(f32[32,1024]{1,0:T(8,128)} %bitcast.11), channel_id=1, source_target_pairs={{0,8},{1,3},{2,10},{3,5},{4,12},{5,7},{6,14},{7,1},{8,16},{9,11},{... | collective-permute-start | bytes 393224 | tf_op jit(solution)/shard_map/ppermute | solution.py:41
  2.0 2.5 %collective-permute-start.1 = (f32[32,1024]{1,0:T(8,128)}, f32[32,1024]{1,0:T(8,128)S(1)}, u32[]{:S(2)}, u32[]{:S(2)}) collective-permute-start(f32[32,1024]{1,0:T(8,128)} %bitcast.12), channel_id=1, source_target_pairs={{0,16},{1,5},{2,18},{3,7},{4,20},{5,1},{6,22},{7,3},{8,24},{9,13},... | collective-permute-start | bytes 393224 | tf_op jit(solution)/shard_map/ppermute | solution.py:41
  4.5 1.2 %collective-permute-start.2 = (f32[32,1024]{1,0:T(8,128)}, f32[32,1024]{1,0:T(8,128)S(1)}, u32[]{:S(2)}, u32[]{:S(2)}) collective-permute-start(f32[32,1024]{1,0:T(8,128)} %bitcast.13), channel_id=1, source_target_pairs={{0,24},{1,7},{2,26},{3,1},{4,28},{5,3},{6,30},{7,5},{8,0},{9,15},{... | collective-permute-start | bytes 393224 | tf_op jit(solution)/shard_map/ppermute | solution.py:41
  5.6 0.2 collective-permute-done
  5.9 2.6 %collective-permute-done.1 = f32[32,1024]{1,0:T(8,128)S(1)} collective-permute-done((f32[32,1024]{1,0:T(8,128)}, f32[32,1024]{1,0:T(8,128)S(1)}, u32[]{:S(2)}, u32[]{:S(2)}) %collective-permute-start.1) | collective-permute-done | bytes 131104 | tf_op jit(solution)/shard_map/ppermute | solution.py:41
  8.4 0.1 collective-permute-done.2
  8.5 0.9 %pad_maximum_fusion.mine = f32[4,32,1024]{2,1,0:T(8,128)S(1)} fusion(f32[1,32,1024]{2,1,0:T(8,128)S(1)} %bitcast.16, f32[1,32,1024]{2,1,0:T(8,128)S(1)} %bitcast.15, f32[1,32,1024]{2,1,0:T(8,128)S(1)} %bitcast.14, f32[1,32,1024]{2,1,0:T(8,128)} %param.3), kind=kLoop, calls=%fused_computation | loop fusion | flops 393216 | bytes 1048576 | tf_op jit(solution)/shard_map/stack | solution.py:302
  9.5 4.1 %collective-permute-start.6 = (f32[4,32,1024]{2,1,0:T(8,128)S(1)}, f32[4,32,1024]{2,1,0:T(8,128)S(1)}, u32[]{:S(2)}, u32[]{:S(2)}) collective-permute-start(f32[4,32,1024]{2,1,0:T(8,128)S(1)} %pad_maximum_fusion.mine), channel_id=1, source_target_pairs={{0,6},{1,25},{2,0},{3,27},{4,2},{5,29},{6,4},{7,31},{8,14},{9,1},{... | collective-permute-start | bytes 1572872 | tf_op jit(solution)/shard_map/ppermute | solution.py:41
  13.6 0.0 collective-permute-start.4
  13.6 2.4 %collective-permute-start.3 = (f32[4,32,1024]{2,1,0:T(8,128)S(1)}, f32[4,32,1024]{2,1,0:T(8,128)S(1)}, u32[]{:S(2)}, u32[]{:S(2)}) collective-permute-start(f32[4,32,1024]{2,1,0:T(8,128)S(1)} %pad_maximum_fusion.mine), channel_id=1, source_target_pairs={{0,1},{1,0},{2,3},{3,2},{4,5},{5,4},{6,7},{7,6},{8,9},{9,8},{10,11... | collective-permute-start | bytes 1572872 | tf_op jit(solution)/shard_map/ppermute | solution.py:45
  16.0 3.8 %collective-permute-done.6.mine = f32[4,32,1024]{2,1,0:T(8,128)S(1)} collective-permute-done((f32[4,32,1024]{2,1,0:T(8,128)S(1)}, f32[4,32,1024]{2,1,0:T(8,128)S(1)}, u32[]{:S(2)}, u32[]{:S(2)}) %collective-permute-start.6) | collective-permute-done | bytes 524320 | tf_op jit(solution)/shard_map/ppermute | solution.py:41
  19.7 2.9 %collective-permute-start.7 = (f32[4,32,1024]{2,1,0:T(8,128)S(1)}, f32[4,32,1024]{2,1,0:T(8,128)S(1)}, u32[]{:S(2)}, u32[]{:S(2)}) collective-permute-start(f32[4,32,1024]{2,1,0:T(8,128)S(1)} %collective-permute-done.6.mine), channel_id=1, source_target_pairs={{0,1},{1,0},{2,3},{3,2},{4,5},{5,4},{6,7},{7,6},{8,9},{9,8},{10,11... | collective-permute-start | bytes 1572872 | tf_op jit(solution)/shard_map/ppermute | solution.py:45
  22.7 0.5 collective-permute-done.4.mine
  23.1 3.2 %collective-permute-start.5 = (f32[4,32,1024]{2,1,0:T(8,128)S(1)}, f32[4,32,1024]{2,1,0:T(8,128)S(1)}, u32[]{:S(2)}, u32[]{:S(2)}) collective-permute-start(f32[4,32,1024]{2,1,0:T(8,128)S(1)} %collective-permute-done.4.mine), channel_id=1, source_target_pairs={{0,1},{1,0},{2,3},{3,2},{4,5},{5,4},{6,7},{7,6},{8,9},{9,8},{10,11... | collective-permute-start | bytes 1572872 | tf_op jit(solution)/shard_map/ppermute | solution.py:45
  26.4 1.7 %collective-permute-start.8 = (f32[2,32,1024]{2,1,0:T(8,128)S(1)}, f32[2,32,1024]{2,1,0:T(8,128)S(1)}, u32[]{:S(2)}, u32[]{:S(2)}) collective-permute-start(f32[2,32,1024]{2,1,0:T(8,128)S(1)} %slice.8), channel_id=1, source_target_pairs={{0,4},{1,17},{2,6},{3,19},{4,0},{5,21},{6,2},{7,23},{8,12},{9,25},... | collective-permute-start | bytes 786440 | tf_op jit(solution)/shard_map/ppermute | solution.py:41
  28.1 0.0 collective-permute-done.3.mate
  28.1 0.1 collective-permute-start.9
  28.2 0.0 copy-start
  28.2 0.7 copy-done
  28.9 2.1 %prepare.1 = (bf16[768,1024]{1,0:T(8,128)(2,1)S(1)}, bf16[768,1024]{1,0:T(8,128)(2,1)S(1)}, bf16[384,256]{1,0:T(8,128)(2,1)S(1)}) custom-call(s32[1,256]{1,0:T(1,128)S(1)} %bitcast.9, f32[3,256,1024]{2,1,0:T(8,128)} %bitcast.10), custom_call_target="tpu_custom_call" | custom-call | flops 20000000 | bytes 8388608 | tf_op jit(solution)/shard_map/prepare/pallas_call | solution.py:86
  30.9 4.8 %collective-permute-done.8.refs_3_ = f32[2,32,1024]{2,1,0:T(8,128)S(1)} collective-permute-done((f32[2,32,1024]{2,1,0:T(8,128)S(1)}, f32[2,32,1024]{2,1,0:T(8,128)S(1)}, u32[]{:S(2)}, u32[]{:S(2)}) %collective-permute-start.8) | collective-permute-done | bytes 262176 | tf_op jit(solution)/shard_map/ppermute | solution.py:41
  35.7 0.2 collective-permute-start.11
  35.9 0.6 collective-permute-done.9.refs_6_
  36.4 0.2 collective-permute-start.10
  36.7 1.6 %expand.3.refs_0_ = bf16[8,32,768]{2,1,0:T(8,128)(2,1)S(1)} custom-call(bf16[768,1024]{1,0:T(8,128)(2,1)S(1)} %get-tuple-element.8.high.refs_7_, bf16[768,1024]{1,0:T(8,128)(2,1)S(1)} %get-tuple-element.9.low.refs_8_, f32[4,32,1024]{2,1,0:T(8,128)S(1)} %pad_maximum_fusion.mine, f32[4,32,1024]{2,1,0:T(8,128)S(1)} %collective-permute-done.3.mate), custom_call_target="tpu_custom_call" | custom-call | flops 1200000000 | bytes 1048576 | tf_op jit(solution)/shard_map/expand/pallas_call | solution.py:136
  38.3 1.6 %expand.5.refs_2_ = bf16[8,32,768]{2,1,0:T(8,128)(2,1)S(1)} custom-call(bf16[768,1024]{1,0:T(8,128)(2,1)S(1)} %get-tuple-element.8.high.refs_7_, bf16[768,1024]{1,0:T(8,128)(2,1)S(1)} %get-tuple-element.9.low.refs_8_, f32[4,32,1024]{2,1,0:T(8,128)S(1)} %collective-permute-done.6.mine, f32[4,32,1024]{2,1,0:T(8,128)S(1)} %collective-permute-done.7.mate), custom_call_target="tpu_custom_call" | custom-call | flops 1200000000 | bytes 1048576 | tf_op jit(solution)/shard_map/expand/pallas_call | solution.py:136
  40.0 0.0 collective-permute-done.5.mate
  40.0 1.6 %expand.4.refs_1_ = bf16[8,32,768]{2,1,0:T(8,128)(2,1)S(1)} custom-call(bf16[768,1024]{1,0:T(8,128)(2,1)S(1)} %get-tuple-element.8.high.refs_7_, bf16[768,1024]{1,0:T(8,128)(2,1)S(1)} %get-tuple-element.9.low.refs_8_, f32[4,32,1024]{2,1,0:T(8,128)S(1)} %collective-permute-done.4.mine, f32[4,32,1024]{2,1,0:T(8,128)S(1)} %collective-permute-done.5.mate), custom_call_target="tpu_custom_call" | custom-call | flops 1200000000 | bytes 1048576 | tf_op jit(solution)/shard_map/expand/pallas_call | solution.py:136
  41.6 0.0 collective-permute-done.11.refs_5_
  41.7 4.3 %build.1 = bf16[128,72,128]{2,1,0:T(8,128)(2,1)S(1)} custom-call(bf16[8,32,768]{2,1,0:T(8,128)(2,1)S(1)} %expand.3.refs_0_, bf16[8,32,768]{2,1,0:T(8,128)(2,1)S(1)} %expand.4.refs_1_, bf16[8,32,768]{2,1,0:T(8,128)(2,1)S(1)} %expand.5.refs_2_, f32[2,32,1024]{2,1,0:T(8,128)S(1)} %collective-permute-done.8.refs_3_, ...), custom_call_target="tpu_custom_call" | custom-call | tf_op jit(solution)/shard_map/build/pallas_call | solution.py:214
  46.0 37.7 %all_to_all.5.received = bf16[128,72,128]{2,1,0:T(8,128)(2,1)S(1)} all-to-all(bf16[128,72,128]{2,1,0:T(8,128)(2,1)S(1)} %build.1), channel_id=1, replica_groups=mesh['y'=4,'z'=4,'x'=4,'c'=2] {'c','z','y','x'}, dimensions={0} | all-to-all | bytes 4718592 | tf_op jit(solution)/shard_map/all_to_all | solution.py:317
  83.6 2.3 %settle.1 = bf16[3,384,1024]{2,1,0:T(8,128)(2,1)} custom-call(bf16[128,72,128]{2,1,0:T(8,128)(2,1)S(1)} %all_to_all.5.received), custom_call_target="tpu_custom_call" | custom-call | tf_op jit(solution)/shard_map/settle/pallas_call | solution.py:279
  (4 shorter events, 0.0 us)
Async XLA Ops:
  0.0 5.9 %collective-permute-start = (f32[32,1024]{1,0:T(8,128)}, f32[32,1024]{1,0:T(8,128)S(1)}, u32[]{:S(2)}, u32[]{:S(2)}) collective-permute-start(f32[32,1024]{1,0:T(8,128)} %bitcast.11), channel_id=1, source_target_pairs={{0,8},{1,3},{2,10},{3,5},{4,12},{5,7},{6,14},{7,1},{8,16},{9,11},{... | collective-permute-start | bytes 393224 | tf_op jit(solution)/shard_map/ppermute | solution.py:41
  2.0 6.4 %collective-permute-start.1 = (f32[32,1024]{1,0:T(8,128)}, f32[32,1024]{1,0:T(8,128)S(1)}, u32[]{:S(2)}, u32[]{:S(2)}) collective-permute-start(f32[32,1024]{1,0:T(8,128)} %bitcast.12), channel_id=1, source_target_pairs={{0,16},{1,5},{2,18},{3,7},{4,20},{5,1},{6,22},{7,3},{8,24},{9,13},... | collective-permute-start | bytes 393224 | tf_op jit(solution)/shard_map/ppermute | solution.py:41
  4.5 4.0 %collective-permute-start.2 = (f32[32,1024]{1,0:T(8,128)}, f32[32,1024]{1,0:T(8,128)S(1)}, u32[]{:S(2)}, u32[]{:S(2)}) collective-permute-start(f32[32,1024]{1,0:T(8,128)} %bitcast.13), channel_id=1, source_target_pairs={{0,24},{1,7},{2,26},{3,1},{4,28},{5,3},{6,30},{7,5},{8,0},{9,15},{... | collective-permute-start | bytes 393224 | tf_op jit(solution)/shard_map/ppermute | solution.py:41
  9.5 10.2 %collective-permute-start.6 = (f32[4,32,1024]{2,1,0:T(8,128)S(1)}, f32[4,32,1024]{2,1,0:T(8,128)S(1)}, u32[]{:S(2)}, u32[]{:S(2)}) collective-permute-start(f32[4,32,1024]{2,1,0:T(8,128)S(1)} %pad_maximum_fusion.mine), channel_id=1, source_target_pairs={{0,6},{1,25},{2,0},{3,27},{4,2},{5,29},{6,4},{7,31},{8,14},{9,1},{... | collective-permute-start | bytes 1572872 | tf_op jit(solution)/shard_map/ppermute | solution.py:41
  13.6 9.5 %collective-permute-start.4 = (f32[4,32,1024]{2,1,0:T(8,128)S(1)}, f32[4,32,1024]{2,1,0:T(8,128)S(1)}, u32[]{:S(2)}, u32[]{:S(2)}) collective-permute-start(f32[4,32,1024]{2,1,0:T(8,128)S(1)} %pad_maximum_fusion.mine), channel_id=1, source_target_pairs={{0,2},{1,9},{2,4},{3,11},{4,6},{5,13},{6,0},{7,15},{8,10},{9,17},{... | collective-permute-start | bytes 1572872 | tf_op jit(solution)/shard_map/ppermute | solution.py:41
  13.6 14.5 %collective-permute-start.3 = (f32[4,32,1024]{2,1,0:T(8,128)S(1)}, f32[4,32,1024]{2,1,0:T(8,128)S(1)}, u32[]{:S(2)}, u32[]{:S(2)}) collective-permute-start(f32[4,32,1024]{2,1,0:T(8,128)S(1)} %pad_maximum_fusion.mine), channel_id=1, source_target_pairs={{0,1},{1,0},{2,3},{3,2},{4,5},{5,4},{6,7},{7,6},{8,9},{9,8},{10,11... | collective-permute-start | bytes 1572872 | tf_op jit(solution)/shard_map/ppermute | solution.py:45
  19.7 18.6 %collective-permute-start.7 = (f32[4,32,1024]{2,1,0:T(8,128)S(1)}, f32[4,32,1024]{2,1,0:T(8,128)S(1)}, u32[]{:S(2)}, u32[]{:S(2)}) collective-permute-start(f32[4,32,1024]{2,1,0:T(8,128)S(1)} %collective-permute-done.6.mine), channel_id=1, source_target_pairs={{0,1},{1,0},{2,3},{3,2},{4,5},{5,4},{6,7},{7,6},{8,9},{9,8},{10,11... | collective-permute-start | bytes 1572872 | tf_op jit(solution)/shard_map/ppermute | solution.py:45
  23.1 16.9 %collective-permute-start.5 = (f32[4,32,1024]{2,1,0:T(8,128)S(1)}, f32[4,32,1024]{2,1,0:T(8,128)S(1)}, u32[]{:S(2)}, u32[]{:S(2)}) collective-permute-start(f32[4,32,1024]{2,1,0:T(8,128)S(1)} %collective-permute-done.4.mine), channel_id=1, source_target_pairs={{0,1},{1,0},{2,3},{3,2},{4,5},{5,4},{6,7},{7,6},{8,9},{9,8},{10,11... | collective-permute-start | bytes 1572872 | tf_op jit(solution)/shard_map/ppermute | solution.py:45
  26.4 9.3 %collective-permute-start.8 = (f32[2,32,1024]{2,1,0:T(8,128)S(1)}, f32[2,32,1024]{2,1,0:T(8,128)S(1)}, u32[]{:S(2)}, u32[]{:S(2)}) collective-permute-start(f32[2,32,1024]{2,1,0:T(8,128)S(1)} %slice.8), channel_id=1, source_target_pairs={{0,4},{1,17},{2,6},{3,19},{4,0},{5,21},{6,2},{7,23},{8,12},{9,25},... | collective-permute-start | bytes 786440 | tf_op jit(solution)/shard_map/ppermute | solution.py:41
  28.1 8.4 %collective-permute-start.9 = (f32[2,32,1024]{2,1,0:T(8,128)S(1)}, f32[2,32,1024]{2,1,0:T(8,128)S(1)}, u32[]{:S(2)}, u32[]{:S(2)}) collective-permute-start(f32[2,32,1024]{2,1,0:T(8,128)S(1)} %slice.9), channel_id=1, source_target_pairs={{0,16},{1,5},{2,18},{3,7},{4,20},{5,1},{6,22},{7,3},{8,24},{9,13},... | collective-permute-start | bytes 786440 | tf_op jit(solution)/shard_map/ppermute | solution.py:41
  28.2 0.7 copy-start
  35.7 6.0 %collective-permute-start.11 = (f32[2,32,1024]{2,1,0:T(8,128)S(1)}, f32[2,32,1024]{2,1,0:T(8,128)S(1)}, u32[]{:S(2)}, u32[]{:S(2)}) collective-permute-start(f32[2,32,1024]{2,1,0:T(8,128)S(1)} %collective-permute-done.8.refs_3_), channel_id=1, source_target_pairs={{0,1},{1,0},{2,3},{3,2},{4,5},{5,4},{6,7},{7,6},{8,9},{9,8},{10,11... | collective-permute-start | bytes 786440 | tf_op jit(solution)/shard_map/ppermute | solution.py:45
  36.4 5.2 %collective-permute-start.10 = (f32[2,32,1024]{2,1,0:T(8,128)S(1)}, f32[2,32,1024]{2,1,0:T(8,128)S(1)}, u32[]{:S(2)}, u32[]{:S(2)}) collective-permute-start(f32[2,32,1024]{2,1,0:T(8,128)S(1)} %collective-permute-done.9.refs_6_), channel_id=1, source_target_pairs={{0,1},{1,0},{2,3},{3,2},{4,5},{5,4},{6,7},{7,6},{8,9},{9,8},{10,11... | collective-permute-start | bytes 786440 | tf_op jit(solution)/shard_map/ppermute | solution.py:45

commit v3 on v2

--- a/solution.py
+++ b/solution.py
@@ -148,9 +148,9 @@
 
 
 def build_kernel(points, rows, *refs):
-    lines, pieces = refs[:3], refs[3:7]
-    high, low, picks_in, message = refs[7:11]
-    table, picks, chunk, spread, in_sems = refs[11:]
+    lines, pieces = refs[:3], refs[3:5]
+    high, low, picks_in, message = refs[5:9]
+    table, picks, spread, in_sems = refs[9:]
     z, x, c = lax.axis_index("z"), lax.axis_index("x"), lax.axis_index("c")
     copies = [
         pltpu.make_async_copy(line, table.at[k], in_sems.at[i])
@@ -168,12 +168,14 @@
 
     def step(i, _):
         dz = lax.rem(z - i + SIDE, SIDE)
+        found = []
         for column in range(SIDE):
             dx = lax.rem(x - column + SIDE, SIDE)
             for core in range(2):
                 k, inner = (dx, dz) if core == 0 else (dz, dx)
                 side = jnp.where(c == core, 0, SIDE)
-                chunk[pl.ds((column * 2 + core) * rows, rows), :] = table[k, side + inner]
+                found.append(table[k, side + inner])
+        chunk = jnp.concatenate(found, axis=0)
         for comp in range(COMPS):
             moved = lax.dot_general(
                 picks[...],
@@ -214,12 +216,11 @@
     return pl.pallas_call(
         functools.partial(build_kernel, points, rows),
         out_shape=jax.ShapeDtypeStruct(sent, jnp.bfloat16),
-        in_specs=[remote] * 3 + [whole] * 6 + [remote],
+        in_specs=[remote] * 3 + [whole] * 4 + [remote],
         out_specs=whole,
         scratch_shapes=[
             pltpu.VMEM((SIDE, 8, rows, wide), jnp.bfloat16),
             pltpu.VMEM(picks.shape, jnp.bfloat16),
-            pltpu.VMEM((8 * rows, wide), jnp.bfloat16),
             pltpu.VMEM((CAP * COMPS, DEVICES * 8, LANES), jnp.float32),
             pltpu.SemaphoreType.DMA((4,)),
         ],
@@ -228,31 +229,32 @@
     )(*lines, *pieces, high, low, picks)
 
 
-def settle_kernel(count, received, out, wide, narrow, ready, out_sems):
+def settle_kernel(count, received, out, wides, narrows, ready, out_sems):
     parts = DEVICES // count
     planes = count // (2 * SIDE)
 
     def lines(i):
-        return pl.ds(pl.multiple_of(i * count * CAP, count * CAP), count * CAP)
+        return pl.ds(i * count * CAP, count * CAP)
 
     def leave(i):
         return pltpu.make_async_copy(ready.at[:, lines(i)], out.at[:, lines(i)], out_sems.at[i])
 
-    def step(i, _):
+    def step(i):
         for core in range(2):
             for plane in range(planes):
-                y, z = (i * planes + plane) // SIDE, lax.rem(i * planes + plane, SIDE)
+                y, z = divmod(i * planes + plane, SIDE)
                 run = received[pl.ds(position(y, z, 0, core), SIDE)]
-                wide[pl.ds((core * planes + plane) * SIDE * 72, SIDE * 72), :] = run.reshape(
+                wides[i % 2, pl.ds((core * planes + plane) * SIDE * 72, SIDE * 72), :] = run.reshape(
                     SIDE * 72, LANES
                 ).astype(jnp.float32)
         for comp in range(COMPS):
             for j in range(8):
                 for r in range(CAP):
                     for core in range(2):
-                        narrow[
-                            comp * 8 + j, pl.ds(core * CAP + r, count // 2, stride=2 * CAP), :
-                        ] = wide[
+                        narrows[
+                            i % 2, comp * 8 + j, pl.ds(core * CAP + r, count // 2, stride=2 * CAP), :
+                        ] = wides[
+                            i % 2,
                             pl.ds(
                                 core * count // 2 * 72 + (r * COMPS + comp) * 8 + j,
                                 count // 2,
@@ -262,13 +264,14 @@
                         ]
         for comp in range(COMPS):
             for j in range(8):
-                ready[comp, lines(i), j * LANES : (j + 1) * LANES] = narrow[comp * 8 + j].astype(
+                ready[comp, lines(i), j * LANES : (j + 1) * LANES] = narrows[i % 2, comp * 8 + j].astype(
                     jnp.bfloat16
                 )
         leave(i).start()
         return 0
 
-    lax.fori_loop(0, parts, step, 0)
+    for i in range(parts):
+        step(i)
     for i in range(parts):
         leave(i).wait()
 
@@ -282,8 +285,8 @@
         in_specs=[pl.BlockSpec(memory_space=pltpu.VMEM)],
         out_specs=pl.BlockSpec(memory_space=pl.ANY),
         scratch_shapes=[
-            pltpu.VMEM((count * 72, LANES), jnp.float32),
-            pltpu.VMEM((COMPS * 8, count * CAP, LANES), jnp.float32),
+            pltpu.VMEM((2, count * 72, LANES), jnp.float32),
+            pltpu.VMEM((2, COMPS * 8, count * CAP, LANES), jnp.float32),
             pltpu.VMEM(shape, jnp.bfloat16),
             pltpu.SemaphoreType.DMA((DEVICES // count,)),
         ],
@@ -299,7 +302,7 @@
     near = [own]
     for k in range(1, SIDE):
         near.append(turn(own, "z", "x", k))
-    line = lax.optimization_barrier(jnp.stack(near))
+    line = jnp.stack(near)
     mate = partner(line)
 
     def far(array, first, second, k):
@@ -311,9 +314,7 @@
     for k in (1, 3):
         moved, swapped = far(line, "x", "z", k)
         lines.append(expand(moved, swapped, high, low, points))
-    a, a_swapped = far(line[:2], "x", "z", 2)
-    b, b_swapped = far(mate[2:], "z", "x", 2)
-    message = build(lines, (a, b_swapped, a_swapped, b), high, low, picks)
+    message = build(lines, far(line, "x", "z", 2), high, low, picks)
     received = lax.all_to_all(message, ("c", "z", "y", "x"), split_axis=0, concat_axis=0, tiled=True)
     return jnp.transpose(settle(received), (1, 0, 2))
 

time: 86.1 us -> 83.8 us (0.973)
  waiting for transfers between devices: 12.4 us -> 10.4 us
    ppermute x7 -> x6, waiting for transfers between devices: 12.4 us -> 10.4 us  [turn(): return lax.ppermute(array, ('z', 'x', 'c'), pairs)]
    ppermute x5 -> x4, starting transfers between devices: 8.96 us -> 9.56 us  [partner(): lax.ppermute(array, ('z', 'x', 'c'), [(i, i ^ 1) for i in range(2 * SIDE...]
    ppermute x7 -> x6, starting transfers between devices: 11.5 us -> 11.1 us  [turn(): return lax.ppermute(array, ('z', 'x', 'c'), pairs)]
  transfers between devices with their start and end apart: 12 -> 10, of which waited for: 7 -> 5; matrix products, arithmetic and copies ran while one was open for 0% -> 0% of each run, Pallas kernels for 8% -> 8%
where the time goes in v3:
time: 83.8 us; the launch traced here: 83.6 us
  blocking collectives  37.3 us (45%)
  starting transfers between devices  20.6 us (25%)
  Pallas kernels  13.5 us (16%)
  waiting for transfers between devices  10.4 us (12%)
  other arithmetic  0.95 us (1%)
    all_to_all x1, blocking collectives, steps(): lax.all_to_all(message, ('c', 'z', 'y', 'x'), split_axis=0, concat_axis=0...  37.3 us
    ppermute x6, starting transfers between devices, turn(): return lax.ppermute(array, ('z', 'x', 'c'), pairs)  11.1 us
    ppermute x6, waiting for transfers between devices, turn(): return lax.ppermute(array, ('z', 'x', 'c'), pairs)  10.4 us
    ppermute x4, starting transfers between devices, partner(): lax.ppermute(array, ('z', 'x', 'c'), [(i, i ^ 1) for i in range(2 * SIDE...  9.56 us
    pallas_call x3, Pallas kernels, expand(): pl.pallas_call(functools.partial(expand_kernel, points), out_shape=jax.Sh...  4.93 us
    pallas_call x1, Pallas kernels, build(): pl.pallas_call(functools.partial(build_kernel, points, rows), out_shape=j...  4.28 us
    pallas_call x1, Pallas kernels, settle(): pl.pallas_call(functools.partial(settle_kernel, count), out_shape=jax.Sha...  2.27 us
    pallas_call x1, Pallas kernels, prepare(): pl.pallas_call(functools.partial(prepare_kernel, points), out_shape=(half...  2.05 us
  transfers between devices with their start and end apart: 10, of which 5 were waited for; matrix products, arithmetic and copies ran while one was open for 0% of the time, Pallas kernels for 8%

profile of v3, /device:TPU:1, one launch (start us, length us, event | category | flops | bytes accessed | tf_op | source)
XLA Modules:
  0.0 83.6 jit_solution(4526127162968942477)
XLA Ops:
  0.0 2.0 %collective-permute-start = (f32[32,1024]{1,0:T(8,128)}, f32[32,1024]{1,0:T(8,128)S(1)}, u32[]{:S(2)}, u32[]{:S(2)}) collective-permute-start(f32[32,1024]{1,0:T(8,128)} %bitcast.11), channel_id=1, source_target_pairs={{0,8},{1,3},{2,10},{3,5},{4,12},{5,7},{6,14},{7,1},{8,16},{9,11},{... | collective-permute-start | bytes 393224 | tf_op jit(solution)/shard_map/ppermute | solution.py:41
  2.0 2.5 %collective-permute-start.1 = (f32[32,1024]{1,0:T(8,128)}, f32[32,1024]{1,0:T(8,128)S(1)}, u32[]{:S(2)}, u32[]{:S(2)}) collective-permute-start(f32[32,1024]{1,0:T(8,128)} %bitcast.12), channel_id=1, source_target_pairs={{0,16},{1,5},{2,18},{3,7},{4,20},{5,1},{6,22},{7,3},{8,24},{9,13},... | collective-permute-start | bytes 393224 | tf_op jit(solution)/shard_map/ppermute | solution.py:41
  4.5 1.2 %collective-permute-start.2 = (f32[32,1024]{1,0:T(8,128)}, f32[32,1024]{1,0:T(8,128)S(1)}, u32[]{:S(2)}, u32[]{:S(2)}) collective-permute-start(f32[32,1024]{1,0:T(8,128)} %bitcast.13), channel_id=1, source_target_pairs={{0,24},{1,7},{2,26},{3,1},{4,28},{5,3},{6,30},{7,5},{8,0},{9,15},{... | collective-permute-start | bytes 393224 | tf_op jit(solution)/shard_map/ppermute | solution.py:41
  5.6 0.2 collective-permute-done
  5.9 2.6 %collective-permute-done.1 = f32[32,1024]{1,0:T(8,128)S(1)} collective-permute-done((f32[32,1024]{1,0:T(8,128)}, f32[32,1024]{1,0:T(8,128)S(1)}, u32[]{:S(2)}, u32[]{:S(2)}) %collective-permute-start.1) | collective-permute-done | bytes 131104 | tf_op jit(solution)/shard_map/ppermute | solution.py:41
  8.4 0.1 collective-permute-done.2
  8.5 0.9 %pad_maximum_fusion.mine = f32[4,32,1024]{2,1,0:T(8,128)S(1)} fusion(f32[1,32,1024]{2,1,0:T(8,128)S(1)} %bitcast.16, f32[1,32,1024]{2,1,0:T(8,128)S(1)} %bitcast.15, f32[1,32,1024]{2,1,0:T(8,128)S(1)} %bitcast.14, f32[1,32,1024]{2,1,0:T(8,128)} %param.3), kind=kLoop, calls=%fused_computation | loop fusion | flops 393216 | bytes 1048576 | tf_op jit(solution)/shard_map/stack | solution.py:305
  9.5 4.1 %collective-permute-start.6 = (f32[4,32,1024]{2,1,0:T(8,128)S(1)}, f32[4,32,1024]{2,1,0:T(8,128)S(1)}, u32[]{:S(2)}, u32[]{:S(2)}) collective-permute-start(f32[4,32,1024]{2,1,0:T(8,128)S(1)} %pad_maximum_fusion.mine), channel_id=1, source_target_pairs={{0,6},{1,25},{2,0},{3,27},{4,2},{5,29},{6,4},{7,31},{8,14},{9,1},{... | collective-permute-start | bytes 1572872 | tf_op jit(solution)/shard_map/ppermute | solution.py:41
  13.6 0.0 collective-permute-start.4
  13.6 1.3 %collective-permute-start.8 = (f32[4,32,1024]{2,1,0:T(8,128)S(1)}, f32[4,32,1024]{2,1,0:T(8,128)S(1)}, u32[]{:S(2)}, u32[]{:S(2)}) collective-permute-start(f32[4,32,1024]{2,1,0:T(8,128)S(1)} %pad_maximum_fusion.mine), channel_id=1, source_target_pairs={{0,4},{1,17},{2,6},{3,19},{4,0},{5,21},{6,2},{7,23},{8,12},{9,25},... | collective-permute-start | bytes 1572872 | tf_op jit(solution)/shard_map/ppermute | solution.py:41
  14.9 3.4 %collective-permute-start.3 = (f32[4,32,1024]{2,1,0:T(8,128)S(1)}, f32[4,32,1024]{2,1,0:T(8,128)S(1)}, u32[]{:S(2)}, u32[]{:S(2)}) collective-permute-start(f32[4,32,1024]{2,1,0:T(8,128)S(1)} %pad_maximum_fusion.mine), channel_id=1, source_target_pairs={{0,1},{1,0},{2,3},{3,2},{4,5},{5,4},{6,7},{7,6},{8,9},{9,8},{10,11... | collective-permute-start | bytes 1572872 | tf_op jit(solution)/shard_map/ppermute | solution.py:45
  18.2 7.1 %collective-permute-done.6.mine = f32[4,32,1024]{2,1,0:T(8,128)S(1)} collective-permute-done((f32[4,32,1024]{2,1,0:T(8,128)S(1)}, f32[4,32,1024]{2,1,0:T(8,128)S(1)}, u32[]{:S(2)}, u32[]{:S(2)}) %collective-permute-start.6) | collective-permute-done | bytes 524320 | tf_op jit(solution)/shard_map/ppermute | solution.py:41
  25.3 3.0 %collective-permute-start.7 = (f32[4,32,1024]{2,1,0:T(8,128)S(1)}, f32[4,32,1024]{2,1,0:T(8,128)S(1)}, u32[]{:S(2)}, u32[]{:S(2)}) collective-permute-start(f32[4,32,1024]{2,1,0:T(8,128)S(1)} %collective-permute-done.6.mine), channel_id=1, source_target_pairs={{0,1},{1,0},{2,3},{3,2},{4,5},{5,4},{6,7},{7,6},{8,9},{9,8},{10,11... | collective-permute-start | bytes 1572872 | tf_op jit(solution)/shard_map/ppermute | solution.py:45
  28.3 0.4 collective-permute-done.4.mine
  28.7 3.2 %collective-permute-start.5 = (f32[4,32,1024]{2,1,0:T(8,128)S(1)}, f32[4,32,1024]{2,1,0:T(8,128)S(1)}, u32[]{:S(2)}, u32[]{:S(2)}) collective-permute-start(f32[4,32,1024]{2,1,0:T(8,128)S(1)} %collective-permute-done.4.mine), channel_id=1, source_target_pairs={{0,1},{1,0},{2,3},{3,2},{4,5},{5,4},{6,7},{7,6},{8,9},{9,8},{10,11... | collective-permute-start | bytes 1572872 | tf_op jit(solution)/shard_map/ppermute | solution.py:45
  32.0 0.0 collective-permute-done.8.refs_3_
  32.0 0.0 collective-permute-start.9
  32.0 0.0 copy-start
  32.0 0.7 copy-done
  32.6 2.1 %prepare.1 = (bf16[768,1024]{1,0:T(8,128)(2,1)S(1)}, bf16[768,1024]{1,0:T(8,128)(2,1)S(1)}, bf16[384,256]{1,0:T(8,128)(2,1)S(1)}) custom-call(s32[1,256]{1,0:T(1,128)S(1)} %bitcast.9, f32[3,256,1024]{2,1,0:T(8,128)} %bitcast.10), custom_call_target="tpu_custom_call" | custom-call | flops 20000000 | bytes 8388608 | tf_op jit(solution)/shard_map/prepare/pallas_call | solution.py:86
  34.7 0.0 collective-permute-done.3.mate
  34.7 1.6 %expand.3.refs_0_ = bf16[8,32,768]{2,1,0:T(8,128)(2,1)S(1)} custom-call(bf16[768,1024]{1,0:T(8,128)(2,1)S(1)} %get-tuple-element.8.high.refs_5_, bf16[768,1024]{1,0:T(8,128)(2,1)S(1)} %get-tuple-element.9.low.refs_6_, f32[4,32,1024]{2,1,0:T(8,128)S(1)} %pad_maximum_fusion.mine, f32[4,32,1024]{2,1,0:T(8,128)S(1)} %collective-permute-done.3.mate), custom_call_target="tpu_custom_call" | custom-call | flops 1200000000 | bytes 1048576 | tf_op jit(solution)/shard_map/expand/pallas_call | solution.py:136
  36.4 0.0 collective-permute-done.7.mate
  36.4 1.6 %expand.5.refs_2_ = bf16[8,32,768]{2,1,0:T(8,128)(2,1)S(1)} custom-call(bf16[768,1024]{1,0:T(8,128)(2,1)S(1)} %get-tuple-element.8.high.refs_5_, bf16[768,1024]{1,0:T(8,128)(2,1)S(1)} %get-tuple-element.9.low.refs_6_, f32[4,32,1024]{2,1,0:T(8,128)S(1)} %collective-permute-done.6.mine, f32[4,32,1024]{2,1,0:T(8,128)S(1)} %collective-permute-done.7.mate), custom_call_target="tpu_custom_call" | custom-call | flops 1200000000 | bytes 1048576 | tf_op jit(solution)/shard_map/expand/pallas_call | solution.py:136
  38.0 0.0 collective-permute-done.5.mate
  38.0 1.6 %expand.4.refs_1_ = bf16[8,32,768]{2,1,0:T(8,128)(2,1)S(1)} custom-call(bf16[768,1024]{1,0:T(8,128)(2,1)S(1)} %get-tuple-element.8.high.refs_5_, bf16[768,1024]{1,0:T(8,128)(2,1)S(1)} %get-tuple-element.9.low.refs_6_, f32[4,32,1024]{2,1,0:T(8,128)S(1)} %collective-permute-done.4.mine, f32[4,32,1024]{2,1,0:T(8,128)S(1)} %collective-permute-done.5.mate), custom_call_target="tpu_custom_call" | custom-call | flops 1200000000 | bytes 1048576 | tf_op jit(solution)/shard_map/expand/pallas_call | solution.py:136
  39.7 0.0 collective-permute-done.9.refs_4_
  39.7 4.3 %build.1 = bf16[128,72,128]{2,1,0:T(8,128)(2,1)S(1)} custom-call(bf16[8,32,768]{2,1,0:T(8,128)(2,1)S(1)} %expand.3.refs_0_, bf16[8,32,768]{2,1,0:T(8,128)(2,1)S(1)} %expand.4.refs_1_, bf16[8,32,768]{2,1,0:T(8,128)(2,1)S(1)} %expand.5.refs_2_, f32[4,32,1024]{2,1,0:T(8,128)S(1)} %collective-permute-done.8.refs_3_, ...), custom_call_target="tpu_custom_call" | custom-call | tf_op jit(solution)/shard_map/build/pallas_call | solution.py:216
  44.0 37.3 %all_to_all.5.received = bf16[128,72,128]{2,1,0:T(8,128)(2,1)S(1)} all-to-all(bf16[128,72,128]{2,1,0:T(8,128)(2,1)S(1)} %build.1), channel_id=1, replica_groups=mesh['y'=4,'z'=4,'x'=4,'c'=2] {'c','z','y','x'}, dimensions={0} | all-to-all | bytes 4718592 | tf_op jit(solution)/shard_map/all_to_all | solution.py:318
  81.3 2.3 %settle.1 = bf16[3,384,1024]{2,1,0:T(8,128)(2,1)} custom-call(bf16[128,72,128]{2,1,0:T(8,128)(2,1)S(1)} %all_to_all.5.received), custom_call_target="tpu_custom_call" | custom-call | tf_op jit(solution)/shard_map/settle/pallas_call | solution.py:282
Async XLA Ops:
  0.0 5.9 %collective-permute-start = (f32[32,1024]{1,0:T(8,128)}, f32[32,1024]{1,0:T(8,128)S(1)}, u32[]{:S(2)}, u32[]{:S(2)}) collective-permute-start(f32[32,1024]{1,0:T(8,128)} %bitcast.11), channel_id=1, source_target_pairs={{0,8},{1,3},{2,10},{3,5},{4,12},{5,7},{6,14},{7,1},{8,16},{9,11},{... | collective-permute-start | bytes 393224 | tf_op jit(solution)/shard_map/ppermute | solution.py:41
  2.0 6.4 %collective-permute-start.1 = (f32[32,1024]{1,0:T(8,128)}, f32[32,1024]{1,0:T(8,128)S(1)}, u32[]{:S(2)}, u32[]{:S(2)}) collective-permute-start(f32[32,1024]{1,0:T(8,128)} %bitcast.12), channel_id=1, source_target_pairs={{0,16},{1,5},{2,18},{3,7},{4,20},{5,1},{6,22},{7,3},{8,24},{9,13},... | collective-permute-start | bytes 393224 | tf_op jit(solution)/shard_map/ppermute | solution.py:41
  4.5 4.0 %collective-permute-start.2 = (f32[32,1024]{1,0:T(8,128)}, f32[32,1024]{1,0:T(8,128)S(1)}, u32[]{:S(2)}, u32[]{:S(2)}) collective-permute-start(f32[32,1024]{1,0:T(8,128)} %bitcast.13), channel_id=1, source_target_pairs={{0,24},{1,7},{2,26},{3,1},{4,28},{5,3},{6,30},{7,5},{8,0},{9,15},{... | collective-permute-start | bytes 393224 | tf_op jit(solution)/shard_map/ppermute | solution.py:41
  9.5 15.9 %collective-permute-start.6 = (f32[4,32,1024]{2,1,0:T(8,128)S(1)}, f32[4,32,1024]{2,1,0:T(8,128)S(1)}, u32[]{:S(2)}, u32[]{:S(2)}) collective-permute-start(f32[4,32,1024]{2,1,0:T(8,128)S(1)} %pad_maximum_fusion.mine), channel_id=1, source_target_pairs={{0,6},{1,25},{2,0},{3,27},{4,2},{5,29},{6,4},{7,31},{8,14},{9,1},{... | collective-permute-start | bytes 1572872 | tf_op jit(solution)/shard_map/ppermute | solution.py:41
  13.6 15.2 %collective-permute-start.4 = (f32[4,32,1024]{2,1,0:T(8,128)S(1)}, f32[4,32,1024]{2,1,0:T(8,128)S(1)}, u32[]{:S(2)}, u32[]{:S(2)}) collective-permute-start(f32[4,32,1024]{2,1,0:T(8,128)S(1)} %pad_maximum_fusion.mine), channel_id=1, source_target_pairs={{0,2},{1,9},{2,4},{3,11},{4,6},{5,13},{6,0},{7,15},{8,10},{9,17},{... | collective-permute-start | bytes 1572872 | tf_op jit(solution)/shard_map/ppermute | solution.py:41
  13.6 18.4 %collective-permute-start.8 = (f32[4,32,1024]{2,1,0:T(8,128)S(1)}, f32[4,32,1024]{2,1,0:T(8,128)S(1)}, u32[]{:S(2)}, u32[]{:S(2)}) collective-permute-start(f32[4,32,1024]{2,1,0:T(8,128)S(1)} %pad_maximum_fusion.mine), channel_id=1, source_target_pairs={{0,4},{1,17},{2,6},{3,19},{4,0},{5,21},{6,2},{7,23},{8,12},{9,25},... | collective-permute-start | bytes 1572872 | tf_op jit(solution)/shard_map/ppermute | solution.py:41
  14.9 19.8 %collective-permute-start.3 = (f32[4,32,1024]{2,1,0:T(8,128)S(1)}, f32[4,32,1024]{2,1,0:T(8,128)S(1)}, u32[]{:S(2)}, u32[]{:S(2)}) collective-permute-start(f32[4,32,1024]{2,1,0:T(8,128)S(1)} %pad_maximum_fusion.mine), channel_id=1, source_target_pairs={{0,1},{1,0},{2,3},{3,2},{4,5},{5,4},{6,7},{7,6},{8,9},{9,8},{10,11... | collective-permute-start | bytes 1572872 | tf_op jit(solution)/shard_map/ppermute | solution.py:45
  25.3 11.0 %collective-permute-start.7 = (f32[4,32,1024]{2,1,0:T(8,128)S(1)}, f32[4,32,1024]{2,1,0:T(8,128)S(1)}, u32[]{:S(2)}, u32[]{:S(2)}) collective-permute-start(f32[4,32,1024]{2,1,0:T(8,128)S(1)} %collective-permute-done.6.mine), channel_id=1, source_target_pairs={{0,1},{1,0},{2,3},{3,2},{4,5},{5,4},{6,7},{7,6},{8,9},{9,8},{10,11... | collective-permute-start | bytes 1572872 | tf_op jit(solution)/shard_map/ppermute | solution.py:45
  28.7 9.3 %collective-permute-start.5 = (f32[4,32,1024]{2,1,0:T(8,128)S(1)}, f32[4,32,1024]{2,1,0:T(8,128)S(1)}, u32[]{:S(2)}, u32[]{:S(2)}) collective-permute-start(f32[4,32,1024]{2,1,0:T(8,128)S(1)} %collective-permute-done.4.mine), channel_id=1, source_target_pairs={{0,1},{1,0},{2,3},{3,2},{4,5},{5,4},{6,7},{7,6},{8,9},{9,8},{10,11... | collective-permute-start | bytes 1572872 | tf_op jit(solution)/shard_map/ppermute | solution.py:45
  32.0 7.7 %collective-permute-start.9 = (f32[4,32,1024]{2,1,0:T(8,128)S(1)}, f32[4,32,1024]{2,1,0:T(8,128)S(1)}, u32[]{:S(2)}, u32[]{:S(2)}) collective-permute-start(f32[4,32,1024]{2,1,0:T(8,128)S(1)} %collective-permute-done.8.refs_3_), channel_id=1, source_target_pairs={{0,1},{1,0},{2,3},{3,2},{4,5},{5,4},{6,7},{7,6},{8,9},{9,8},{10,11... | collective-permute-start | bytes 1572872 | tf_op jit(solution)/shard_map/ppermute | solution.py:45
  32.0 0.7 copy-start

commit v4 on v3

--- a/solution.py
+++ b/solution.py
@@ -154,12 +154,12 @@
     z, x, c = lax.axis_index("z"), lax.axis_index("x"), lax.axis_index("c")
     copies = [
         pltpu.make_async_copy(line, table.at[k], in_sems.at[i])
-        for i, (line, k) in enumerate(zip(lines, (0, 1, 3)))
+        for i, (line, k) in enumerate(zip(lines, (0, 1, 2)))
     ]
     copies.append(pltpu.make_async_copy(picks_in, picks, in_sems.at[3]))
     for copy in copies:
         copy.start()
-    product(points, gathered(pieces), high, low, table.at[2])
+    product(points, gathered(pieces), high, low, table.at[3])
     for copy in copies:
         copy.wait()
 
@@ -311,10 +311,10 @@
 
     lines = []
     lines.append(expand(line, mate, high, low, points))
-    for k in (1, 3):
+    for k in (1, 2):
         moved, swapped = far(line, "x", "z", k)
         lines.append(expand(moved, swapped, high, low, points))
-    message = build(lines, far(line, "x", "z", 2), high, low, picks)
+    message = build(lines, far(line, "x", "z", 3), high, low, picks)
     received = lax.all_to_all(message, ("c", "z", "y", "x"), split_axis=0, concat_axis=0, tiled=True)
     return jnp.transpose(settle(received), (1, 0, 2))
 

time: 83.8 us -> 83.1 us (level)
  waiting for transfers between devices: 10.4 us -> 5.69 us
  starting transfers between devices: 20.6 us -> 23 us
  blocking collectives: 37.3 us -> 39 us
    ppermute x6, waiting for transfers between devices: 10.4 us -> 5.68 us  [turn(): return lax.ppermute(array, ('z', 'x', 'c'), pairs)]
    all_to_all x1, blocking collectives: 37.3 us -> 39 us  [steps(): lax.all_to_all(message, ('c', 'z', 'y', 'x'), split_axis=0, concat_axis=0...]
    ppermute x6, starting transfers between devices: 11.1 us -> 12.3 us  [turn(): return lax.ppermute(array, ('z', 'x', 'c'), pairs)]
    ppermute x4, starting transfers between devices: 9.56 us -> 10.7 us  [partner(): lax.ppermute(array, ('z', 'x', 'c'), [(i, i ^ 1) for i in range(2 * SIDE...]
where the time goes in v4:
time: 83.1 us; the launch traced here: 82.9 us
  blocking collectives  39 us (47%)
  starting transfers between devices  23 us (28%)
  Pallas kernels  13.5 us (16%)
  waiting for transfers between devices  5.69 us (7%)
  other arithmetic  0.95 us (1%)
    all_to_all x1, blocking collectives, steps(): lax.all_to_all(message, ('c', 'z', 'y', 'x'), split_axis=0, concat_axis=0...  39 us
    ppermute x6, starting transfers between devices, turn(): return lax.ppermute(array, ('z', 'x', 'c'), pairs)  12.3 us
    ppermute x4, starting transfers between devices, partner(): lax.ppermute(array, ('z', 'x', 'c'), [(i, i ^ 1) for i in range(2 * SIDE...  10.7 us
    ppermute x6, waiting for transfers between devices, turn(): return lax.ppermute(array, ('z', 'x', 'c'), pairs)  5.68 us
    pallas_call x3, Pallas kernels, expand(): pl.pallas_call(functools.partial(expand_kernel, points), out_shape=jax.Sh...  4.92 us
    pallas_call x1, Pallas kernels, build(): pl.pallas_call(functools.partial(build_kernel, points, rows), out_shape=j...  4.28 us
    pallas_call x1, Pallas kernels, settle(): pl.pallas_call(functools.partial(settle_kernel, count), out_shape=jax.Sha...  2.27 us
    pallas_call x1, Pallas kernels, prepare(): pl.pallas_call(functools.partial(prepare_kernel, points), out_shape=(half...  2.05 us
  transfers between devices with their start and end apart: 10, of which 5 were waited for; matrix products, arithmetic and copies ran while one was open for 0% of the time, Pallas kernels for 8%

profile of v4, /device:TPU:1, one launch (start us, length us, event | category | flops | bytes accessed | tf_op | source)
XLA Modules:
  0.0 82.9 jit_solution(15997490250249044652)
XLA Ops:
  0.0 2.0 %collective-permute-start = (f32[32,1024]{1,0:T(8,128)}, f32[32,1024]{1,0:T(8,128)S(1)}, u32[]{:S(2)}, u32[]{:S(2)}) collective-permute-start(f32[32,1024]{1,0:T(8,128)} %bitcast.11), channel_id=1, source_target_pairs={{0,8},{1,3},{2,10},{3,5},{4,12},{5,7},{6,14},{7,1},{8,16},{9,11},{... | collective-permute-start | bytes 393224 | tf_op jit(solution)/shard_map/ppermute | solution.py:41
  2.0 2.5 %collective-permute-start.1 = (f32[32,1024]{1,0:T(8,128)}, f32[32,1024]{1,0:T(8,128)S(1)}, u32[]{:S(2)}, u32[]{:S(2)}) collective-permute-start(f32[32,1024]{1,0:T(8,128)} %bitcast.12), channel_id=1, source_target_pairs={{0,16},{1,5},{2,18},{3,7},{4,20},{5,1},{6,22},{7,3},{8,24},{9,13},... | collective-permute-start | bytes 393224 | tf_op jit(solution)/shard_map/ppermute | solution.py:41
  4.5 1.2 %collective-permute-start.2 = (f32[32,1024]{1,0:T(8,128)}, f32[32,1024]{1,0:T(8,128)S(1)}, u32[]{:S(2)}, u32[]{:S(2)}) collective-permute-start(f32[32,1024]{1,0:T(8,128)} %bitcast.13), channel_id=1, source_target_pairs={{0,24},{1,7},{2,26},{3,1},{4,28},{5,3},{6,30},{7,5},{8,0},{9,15},{... | collective-permute-start | bytes 393224 | tf_op jit(solution)/shard_map/ppermute | solution.py:41
  5.6 0.2 collective-permute-done
  5.9 2.6 %collective-permute-done.1 = f32[32,1024]{1,0:T(8,128)S(1)} collective-permute-done((f32[32,1024]{1,0:T(8,128)}, f32[32,1024]{1,0:T(8,128)S(1)}, u32[]{:S(2)}, u32[]{:S(2)}) %collective-permute-start.1) | collective-permute-done | bytes 131104 | tf_op jit(solution)/shard_map/ppermute | solution.py:41
  8.4 0.1 collective-permute-done.2
  8.5 0.9 %pad_maximum_fusion.mine = f32[4,32,1024]{2,1,0:T(8,128)S(1)} fusion(f32[1,32,1024]{2,1,0:T(8,128)S(1)} %bitcast.16, f32[1,32,1024]{2,1,0:T(8,128)S(1)} %bitcast.15, f32[1,32,1024]{2,1,0:T(8,128)S(1)} %bitcast.14, f32[1,32,1024]{2,1,0:T(8,128)} %param.3), kind=kLoop, calls=%fused_computation | loop fusion | flops 393216 | bytes 1048576 | tf_op jit(solution)/shard_map/stack | solution.py:305
  9.5 4.0 %collective-permute-start.6 = (f32[4,32,1024]{2,1,0:T(8,128)S(1)}, f32[4,32,1024]{2,1,0:T(8,128)S(1)}, u32[]{:S(2)}, u32[]{:S(2)}) collective-permute-start(f32[4,32,1024]{2,1,0:T(8,128)S(1)} %pad_maximum_fusion.mine), channel_id=1, source_target_pairs={{0,4},{1,17},{2,6},{3,19},{4,0},{5,21},{6,2},{7,23},{8,12},{9,25},... | collective-permute-start | bytes 1572872 | tf_op jit(solution)/shard_map/ppermute | solution.py:41
  13.4 0.7 collective-permute-start.4
  14.2 1.9 %collective-permute-start.8 = (f32[4,32,1024]{2,1,0:T(8,128)S(1)}, f32[4,32,1024]{2,1,0:T(8,128)S(1)}, u32[]{:S(2)}, u32[]{:S(2)}) collective-permute-start(f32[4,32,1024]{2,1,0:T(8,128)S(1)} %pad_maximum_fusion.mine), channel_id=1, source_target_pairs={{0,6},{1,25},{2,0},{3,27},{4,2},{5,29},{6,4},{7,31},{8,14},{9,1},{... | collective-permute-start | bytes 1572872 | tf_op jit(solution)/shard_map/ppermute | solution.py:41
  16.1 3.4 %collective-permute-start.3 = (f32[4,32,1024]{2,1,0:T(8,128)S(1)}, f32[4,32,1024]{2,1,0:T(8,128)S(1)}, u32[]{:S(2)}, u32[]{:S(2)}) collective-permute-start(f32[4,32,1024]{2,1,0:T(8,128)S(1)} %pad_maximum_fusion.mine), channel_id=1, source_target_pairs={{0,1},{1,0},{2,3},{3,2},{4,5},{5,4},{6,7},{7,6},{8,9},{9,8},{10,11... | collective-permute-start | bytes 1572872 | tf_op jit(solution)/shard_map/ppermute | solution.py:45
  19.5 0.9 %collective-permute-done.6.mine = f32[4,32,1024]{2,1,0:T(8,128)S(1)} collective-permute-done((f32[4,32,1024]{2,1,0:T(8,128)S(1)}, f32[4,32,1024]{2,1,0:T(8,128)S(1)}, u32[]{:S(2)}, u32[]{:S(2)}) %collective-permute-start.6) | collective-permute-done | bytes 524320 | tf_op jit(solution)/shard_map/ppermute | solution.py:41
  20.3 3.6 %collective-permute-start.7 = (f32[4,32,1024]{2,1,0:T(8,128)S(1)}, f32[4,32,1024]{2,1,0:T(8,128)S(1)}, u32[]{:S(2)}, u32[]{:S(2)}) collective-permute-start(f32[4,32,1024]{2,1,0:T(8,128)S(1)} %collective-permute-done.6.mine), channel_id=1, source_target_pairs={{0,1},{1,0},{2,3},{3,2},{4,5},{5,4},{6,7},{7,6},{8,9},{9,8},{10,11... | collective-permute-start | bytes 1572872 | tf_op jit(solution)/shard_map/ppermute | solution.py:45
  24.0 1.9 %collective-permute-done.4.mine = f32[4,32,1024]{2,1,0:T(8,128)S(1)} collective-permute-done((f32[4,32,1024]{2,1,0:T(8,128)S(1)}, f32[4,32,1024]{2,1,0:T(8,128)S(1)}, u32[]{:S(2)}, u32[]{:S(2)}) %collective-permute-start.4) | collective-permute-done | bytes 524320 | tf_op jit(solution)/shard_map/ppermute | solution.py:41
  25.9 3.6 %collective-permute-start.5 = (f32[4,32,1024]{2,1,0:T(8,128)S(1)}, f32[4,32,1024]{2,1,0:T(8,128)S(1)}, u32[]{:S(2)}, u32[]{:S(2)}) collective-permute-start(f32[4,32,1024]{2,1,0:T(8,128)S(1)} %collective-permute-done.4.mine), channel_id=1, source_target_pairs={{0,1},{1,0},{2,3},{3,2},{4,5},{5,4},{6,7},{7,6},{8,9},{9,8},{10,11... | collective-permute-start | bytes 1572872 | tf_op jit(solution)/shard_map/ppermute | solution.py:45
  29.5 0.0 collective-permute-done.8.refs_3_
  29.5 0.1 collective-permute-start.9
  29.6 0.0 copy-start
  29.6 0.7 copy-done
  30.3 2.1 %prepare.1 = (bf16[768,1024]{1,0:T(8,128)(2,1)S(1)}, bf16[768,1024]{1,0:T(8,128)(2,1)S(1)}, bf16[384,256]{1,0:T(8,128)(2,1)S(1)}) custom-call(s32[1,256]{1,0:T(1,128)S(1)} %bitcast.9, f32[3,256,1024]{2,1,0:T(8,128)} %bitcast.10), custom_call_target="tpu_custom_call" | custom-call | flops 20000000 | bytes 8388608 | tf_op jit(solution)/shard_map/prepare/pallas_call | solution.py:86
  32.4 0.0 collective-permute-done.3.mate
  32.4 1.6 %expand.3.refs_0_ = bf16[8,32,768]{2,1,0:T(8,128)(2,1)S(1)} custom-call(bf16[768,1024]{1,0:T(8,128)(2,1)S(1)} %get-tuple-element.8.high.refs_5_, bf16[768,1024]{1,0:T(8,128)(2,1)S(1)} %get-tuple-element.9.low.refs_6_, f32[4,32,1024]{2,1,0:T(8,128)S(1)} %pad_maximum_fusion.mine, f32[4,32,1024]{2,1,0:T(8,128)S(1)} %collective-permute-done.3.mate), custom_call_target="tpu_custom_call" | custom-call | flops 1200000000 | bytes 1048576 | tf_op jit(solution)/shard_map/expand/pallas_call | solution.py:136
  34.0 0.0 collective-permute-done.7.mate
  34.0 1.6 %expand.5.refs_2_ = bf16[8,32,768]{2,1,0:T(8,128)(2,1)S(1)} custom-call(bf16[768,1024]{1,0:T(8,128)(2,1)S(1)} %get-tuple-element.8.high.refs_5_, bf16[768,1024]{1,0:T(8,128)(2,1)S(1)} %get-tuple-element.9.low.refs_6_, f32[4,32,1024]{2,1,0:T(8,128)S(1)} %collective-permute-done.6.mine, f32[4,32,1024]{2,1,0:T(8,128)S(1)} %collective-permute-done.7.mate), custom_call_target="tpu_custom_call" | custom-call | flops 1200000000 | bytes 1048576 | tf_op jit(solution)/shard_map/expand/pallas_call | solution.py:136
  35.7 0.0 collective-permute-done.5.mate
  35.7 1.6 %expand.4.refs_1_ = bf16[8,32,768]{2,1,0:T(8,128)(2,1)S(1)} custom-call(bf16[768,1024]{1,0:T(8,128)(2,1)S(1)} %get-tuple-element.8.high.refs_5_, bf16[768,1024]{1,0:T(8,128)(2,1)S(1)} %get-tuple-element.9.low.refs_6_, f32[4,32,1024]{2,1,0:T(8,128)S(1)} %collective-permute-done.4.mine, f32[4,32,1024]{2,1,0:T(8,128)S(1)} %collective-permute-done.5.mate), custom_call_target="tpu_custom_call" | custom-call | flops 1200000000 | bytes 1048576 | tf_op jit(solution)/shard_map/expand/pallas_call | solution.py:136
  37.4 0.0 collective-permute-done.9.refs_4_
  37.4 4.3 %build.1 = bf16[128,72,128]{2,1,0:T(8,128)(2,1)S(1)} custom-call(bf16[8,32,768]{2,1,0:T(8,128)(2,1)S(1)} %expand.3.refs_0_, bf16[8,32,768]{2,1,0:T(8,128)(2,1)S(1)} %expand.4.refs_1_, bf16[8,32,768]{2,1,0:T(8,128)(2,1)S(1)} %expand.5.refs_2_, f32[4,32,1024]{2,1,0:T(8,128)S(1)} %collective-permute-done.8.refs_3_, ...), custom_call_target="tpu_custom_call" | custom-call | tf_op jit(solution)/shard_map/build/pallas_call | solution.py:216
  41.6 39.0 %all_to_all.5.received = bf16[128,72,128]{2,1,0:T(8,128)(2,1)S(1)} all-to-all(bf16[128,72,128]{2,1,0:T(8,128)(2,1)S(1)} %build.1), channel_id=1, replica_groups=mesh['y'=4,'z'=4,'x'=4,'c'=2] {'c','z','y','x'}, dimensions={0} | all-to-all | bytes 4718592 | tf_op jit(solution)/shard_map/all_to_all | solution.py:318
  80.7 2.3 %settle.1 = bf16[3,384,1024]{2,1,0:T(8,128)(2,1)} custom-call(bf16[128,72,128]{2,1,0:T(8,128)(2,1)S(1)} %all_to_all.5.received), custom_call_target="tpu_custom_call" | custom-call | tf_op jit(solution)/shard_map/settle/pallas_call | solution.py:282
Async XLA Ops:
  0.0 5.9 %collective-permute-start = (f32[32,1024]{1,0:T(8,128)}, f32[32,1024]{1,0:T(8,128)S(1)}, u32[]{:S(2)}, u32[]{:S(2)}) collective-permute-start(f32[32,1024]{1,0:T(8,128)} %bitcast.11), channel_id=1, source_target_pairs={{0,8},{1,3},{2,10},{3,5},{4,12},{5,7},{6,14},{7,1},{8,16},{9,11},{... | collective-permute-start | bytes 393224 | tf_op jit(solution)/shard_map/ppermute | solution.py:41
  2.0 6.4 %collective-permute-start.1 = (f32[32,1024]{1,0:T(8,128)}, f32[32,1024]{1,0:T(8,128)S(1)}, u32[]{:S(2)}, u32[]{:S(2)}) collective-permute-start(f32[32,1024]{1,0:T(8,128)} %bitcast.12), channel_id=1, source_target_pairs={{0,16},{1,5},{2,18},{3,7},{4,20},{5,1},{6,22},{7,3},{8,24},{9,13},... | collective-permute-start | bytes 393224 | tf_op jit(solution)/shard_map/ppermute | solution.py:41
  4.5 4.0 %collective-permute-start.2 = (f32[32,1024]{1,0:T(8,128)}, f32[32,1024]{1,0:T(8,128)S(1)}, u32[]{:S(2)}, u32[]{:S(2)}) collective-permute-start(f32[32,1024]{1,0:T(8,128)} %bitcast.13), channel_id=1, source_target_pairs={{0,24},{1,7},{2,26},{3,1},{4,28},{5,3},{6,30},{7,5},{8,0},{9,15},{... | collective-permute-start | bytes 393224 | tf_op jit(solution)/shard_map/ppermute | solution.py:41
  9.5 10.9 %collective-permute-start.6 = (f32[4,32,1024]{2,1,0:T(8,128)S(1)}, f32[4,32,1024]{2,1,0:T(8,128)S(1)}, u32[]{:S(2)}, u32[]{:S(2)}) collective-permute-start(f32[4,32,1024]{2,1,0:T(8,128)S(1)} %pad_maximum_fusion.mine), channel_id=1, source_target_pairs={{0,4},{1,17},{2,6},{3,19},{4,0},{5,21},{6,2},{7,23},{8,12},{9,25},... | collective-permute-start | bytes 1572872 | tf_op jit(solution)/shard_map/ppermute | solution.py:41
  13.4 12.5 %collective-permute-start.4 = (f32[4,32,1024]{2,1,0:T(8,128)S(1)}, f32[4,32,1024]{2,1,0:T(8,128)S(1)}, u32[]{:S(2)}, u32[]{:S(2)}) collective-permute-start(f32[4,32,1024]{2,1,0:T(8,128)S(1)} %pad_maximum_fusion.mine), channel_id=1, source_target_pairs={{0,2},{1,9},{2,4},{3,11},{4,6},{5,13},{6,0},{7,15},{8,10},{9,17},{... | collective-permute-start | bytes 1572872 | tf_op jit(solution)/shard_map/ppermute | solution.py:41
  14.2 15.3 %collective-permute-start.8 = (f32[4,32,1024]{2,1,0:T(8,128)S(1)}, f32[4,32,1024]{2,1,0:T(8,128)S(1)}, u32[]{:S(2)}, u32[]{:S(2)}) collective-permute-start(f32[4,32,1024]{2,1,0:T(8,128)S(1)} %pad_maximum_fusion.mine), channel_id=1, source_target_pairs={{0,6},{1,25},{2,0},{3,27},{4,2},{5,29},{6,4},{7,31},{8,14},{9,1},{... | collective-permute-start | bytes 1572872 | tf_op jit(solution)/shard_map/ppermute | solution.py:41
  16.1 16.3 %collective-permute-start.3 = (f32[4,32,1024]{2,1,0:T(8,128)S(1)}, f32[4,32,1024]{2,1,0:T(8,128)S(1)}, u32[]{:S(2)}, u32[]{:S(2)}) collective-permute-start(f32[4,32,1024]{2,1,0:T(8,128)S(1)} %pad_maximum_fusion.mine), channel_id=1, source_target_pairs={{0,1},{1,0},{2,3},{3,2},{4,5},{5,4},{6,7},{7,6},{8,9},{9,8},{10,11... | collective-permute-start | bytes 1572872 | tf_op jit(solution)/shard_map/ppermute | solution.py:45
  20.3 13.7 %collective-permute-start.7 = (f32[4,32,1024]{2,1,0:T(8,128)S(1)}, f32[4,32,1024]{2,1,0:T(8,128)S(1)}, u32[]{:S(2)}, u32[]{:S(2)}) collective-permute-start(f32[4,32,1024]{2,1,0:T(8,128)S(1)} %collective-permute-done.6.mine), channel_id=1, source_target_pairs={{0,1},{1,0},{2,3},{3,2},{4,5},{5,4},{6,7},{7,6},{8,9},{9,8},{10,11... | collective-permute-start | bytes 1572872 | tf_op jit(solution)/shard_map/ppermute | solution.py:45
  25.9 9.8 %collective-permute-start.5 = (f32[4,32,1024]{2,1,0:T(8,128)S(1)}, f32[4,32,1024]{2,1,0:T(8,128)S(1)}, u32[]{:S(2)}, u32[]{:S(2)}) collective-permute-start(f32[4,32,1024]{2,1,0:T(8,128)S(1)} %collective-permute-done.4.mine), channel_id=1, source_target_pairs={{0,1},{1,0},{2,3},{3,2},{4,5},{5,4},{6,7},{7,6},{8,9},{9,8},{10,11... | collective-permute-start | bytes 1572872 | tf_op jit(solution)/shard_map/ppermute | solution.py:45
  29.5 7.8 %collective-permute-start.9 = (f32[4,32,1024]{2,1,0:T(8,128)S(1)}, f32[4,32,1024]{2,1,0:T(8,128)S(1)}, u32[]{:S(2)}, u32[]{:S(2)}) collective-permute-start(f32[4,32,1024]{2,1,0:T(8,128)S(1)} %collective-permute-done.8.refs_3_), channel_id=1, source_target_pairs={{0,1},{1,0},{2,3},{3,2},{4,5},{5,4},{6,7},{7,6},{8,9},{9,8},{10,11... | collective-permute-start | bytes 1572872 | tf_op jit(solution)/shard_map/ppermute | solution.py:45
  29.6 0.7 copy-start
